TPU v7x, 128 devices: a whole 4x4x4 slice. The times are simulated.
128 devices in a mesh: aa: 16 (over y_hi, x, core), col: 8 (over z, y_lo).
Axes of the slice: x: 4, y: 4 (y_hi: 2, y_lo: 2; y = y_hi * 2 + y_lo), z: 4, core: 2. Of those that a mesh axis runs over, the one named last changes fastest.
Arguments:
- fit_ac: float32 [512, 512, 2048], P('aa', 'col'), may hold values from -0.125 to 0.125
- fit_bd: float32 [2048, 1024], P(('aa', 'col')), may hold values from -6 to 6
- amplitudes: float32 [2, 32, 512, 256], P(None, 'aa', 'col'), may hold values from -0.046875 to 0.046875
Outputs:
- residual: float32 [2, 16, 512, 256], P(None, 'col', 'aa')
All inputs are finite; a program needn't handle non-finite values.
Results may differ from a plain program's by a relative error of at most 0.0003.
Values sent between devices are 32-bit elements; how exact they have to be, the bound alone decides.
No kernel may reach another device: no remote copies, remote signals or barrier semaphores. Data moves between devices by JAX's collectives and lax.ppermute only.
A program may use at most 128 MiB of HBM per device.

v0:
```python
import jax
import jax.numpy as jnp
from jax import lax
from jax.sharding import PartitionSpec as P

NB = 16
ND = 32


def in_order(pieces, dim):
    pieces = jnp.moveaxis(pieces, 0, dim)
    dims = pieces.shape
    return pieces.reshape(*dims[:dim], dims[dim] * dims[dim + 1], *dims[dim + 2 :])


def sent_to_all(shard, axis):
    copies = jnp.broadcast_to(shard, (lax.axis_size(axis), *shard.shape))
    return lax.all_to_all(copies, axis, split_axis=0, concat_axis=0, tiled=True)


def gather_directly(shard, axis, dim):
    return in_order(sent_to_all(shard, axis), dim)


def in_blocks(shard, dim, peers):
    dims = shard.shape
    pieces = shard.reshape(*dims[:dim], peers, dims[dim] // peers, *dims[dim + 1 :])
    return jnp.moveaxis(pieces, dim, 0)


def summed_on_arrival(shard, axis, dim):
    peers = lax.axis_size(axis)
    pieces = lax.all_to_all(in_blocks(shard, dim, peers), axis, 0, 0, tiled=True)
    return jnp.sum(pieces, axis=0)


def contract_rows(fitting_rows, piece):
    return jnp.dot(
        fitting_rows, piece, precision=lax.Precision.HIGHEST, preferred_element_type=jnp.float32
    )


def shards(fit_ac, fit_bd, amplitudes):
    a_local, c_local, count_q = fit_ac.shape
    blocks, d_local, pairs = (amplitudes.shape[0], amplitudes.shape[1], amplitudes.shape[3])
    d_size = ND
    b_size = NB
    fitting_ac = fit_ac.reshape(a_local * c_local, count_q)
    grouped = gather_directly(fit_bd, "col", 0)
    integrals = contract_rows(fitting_ac, lax.all_gather(grouped, "aa", axis=0, tiled=True))
    integrals = integrals.reshape(a_local, c_local, blocks, b_size, d_size)
    all_rows = lax.all_gather(amplitudes, "aa", axis=1, tiled=True)
    partial_value = jnp.einsum(
        "kdcp,ackbd->kbap", all_rows, integrals, precision=lax.Precision.HIGHEST
    )
    return summed_on_arrival(partial_value, "col", 1)


def solution(mesh):
    placed = (P("aa", "col", None), P(("aa", "col"), None), P(None, "aa", "col", None))
    return jax.shard_map(
        shards, mesh=mesh, in_specs=placed, out_specs=P(None, "col", "aa", None), check_vma=False
    )
```

profile of v0, /device:TPU:0, one launch (start us, length us, event | category | flops | bytes accessed | tf_op | source)
XLA Modules:
  0.0 281.9 jit_solution(9344583743285278038)
XLA Ops:
  6.5 0.0 all-gather.3.cloned.1.call-start
  6.5 0.9 broadcast_in_dim.3
  7.4 16.4 %all_to_all.10 = f32[8,16,1024]{2,1,0:T(8,128)} all-to-all(f32[8,16,1024]{2,1,0:T(8,128)S(1)} %broadcast_in_dim.3), channel_id=1, replica_groups=mesh['aa'=16,'col'=8] {'col'}, dimensions={0} | all-to-all | bytes 1048576 | tf_op jit(solution)/shard_map/all_to_all | solution.py:18
  23.9 0.0 all-gather.3.cloned.1.call-update
  23.9 0.0 all-gather.5.cloned.1.call-start
  23.9 0.7 all-gather.5.cloned.1.call-update
  24.6 71.2 %all-gather.3.cloned.1.call-done = f32[2048,1024]{1,0:T(8,128)} async-done(((f32[128,1024]{1,0:T(8,128)}), f32[2048,1024]{1,0:T(8,128)}) %all-gather.3.cloned.1.call-update) | async-done | bytes 8388624 | tf_op jit(solution)/shard_map/all_gather | solution.py:50
  95.9 9.1 %copy.7 = f32[1024,2048]{1,0:T(8,128)} copy(f32[1024,2048]{0,1:T(8,128)} %bitcast.30) | data formatting | bytes 16777216 | tf_op jit(solution)/shard_map/dot_general | solution.py:38
  105.0 131.0 %fusion = f32[32,64,2,16,32]{1,3,4,0,2:T(8,128)} fusion(f32[32,64,2048]{2,1,0:T(8,128)} %param.3, f32[2,16,32,2048,1]{3,2,1,0,4:T(8,128)} %bitcast.31), kind=kOutput, calls=%fused_computation | convolution fusion | flops 51539607552 | bytes 33554432 | tf_op jit(solution)/shard_map/dot_general | solution.py:38
  236.0 0.0 all-gather.5.cloned.1.call-done
  236.0 16.4 %fusion.5 = f32[2,16,32,256]{3,1,2,0:T(8,128)S(1)} fusion(f32[32,64,2,16,32]{1,3,4,0,2:T(8,128)} %fusion, f32[2,32,64,256]{3,2,1,0:T(8,128)} %all-gather.5.cloned.1.call-done), kind=kOutput, calls=%fused_computation.5 | convolution fusion | flops 6442450944 | bytes 13631488 | tf_op jit(solution)/shard_map/kdcp,ackbd->kbap/dot_general | solution.py:53
  252.4 0.6 reshape.12
  253.0 0.5 copy.22
  253.6 20.3 %all_to_all.11 = f32[8,2,2,32,256]{4,2,3,1,0:T(2,128)S(1)} all-to-all(f32[8,2,2,32,256]{4,2,3,1,0:T(2,128)S(1)} %bitcast.32), channel_id=1, replica_groups=mesh['aa'=16,'col'=8] {'col'}, dimensions={0} | all-to-all | bytes 2097152 | tf_op jit(solution)/shard_map/all_to_all | solution.py:33
  273.9 0.4 reduce_sum.9
  274.4 0.7 copy.11
Async XLA Ops:
  6.5 89.4 %all-gather.3.cloned.1.call-start = ((), (), s32[]{:S(2)}) async-start(), calls=%async_computation.2 | async-start | bytes 8912896 | tf_op jit(solution)/shard_map/all_gather | solution.py:50
  23.9 212.1 %all-gather.5.cloned.1.call-start = ((), (), s32[]{:S(2)}) async-start(), calls=%async_computation.3 | async-start | bytes 4456448 | tf_op jit(solution)/shard_map/all_gather | solution.py:52
Sparse Core Ops, SparseCore 0:
  24.0 71.8 all-gather.2
  98.4 53.8 all-gather.4
where the time goes:
time: 282 us
  matrix products  147 us (52%)
  waiting for transfers between devices  72 us (26%)
  blocking collectives  36.8 us (13%)
  between operations  13.4 us (5%)
  local copies, waits for them, and re-layouts  11.8 us (4%)
    dot_general x1, matrix products, contract_rows(): jnp.dot(fitting_rows, piece, precision=lax.Precision.HIGHEST, preferred_e...  131 us
    all_gather x1, waiting for transfers between devices, shards(): lax.all_gather(grouped, 'aa', axis=0, tiled=True)  71.2 us
    all_to_all x1, blocking collectives, summed_on_arrival(): lax.all_to_all(in_blocks(shard, dim, peers), axis, 0, 0, tiled=True)  20.3 us
    all_to_all x1, blocking collectives, sent_to_all(): return lax.all_to_all(copies, axis, split_axis=0, concat_axis=0, tiled=True)  16.4 us
    dot_general x1, matrix products, shards(): jnp.einsum('kdcp,ackbd->kbap', all_rows, integrals, precision=lax.Precisi...  16.4 us
    dot_general x1, local copies, waits for them, and re-layouts, contract_rows(): jnp.dot(fitting_rows, piece, precision=lax.Precision.HIGHEST, preferred_e...  9.14 us
  transfers between devices with their start and end apart: 2, of which 1 were waited for; matrix products, arithmetic and copies ran while one was open for 50% of the time, Pallas kernels for 0%

commit v1 on v0

v1 whole, which is shorter than its diff:
```python
import functools

import jax
import jax.numpy as jnp
from jax import lax
from jax.experimental import pallas as pl
from jax.experimental.pallas import tpu as pltpu
from jax.sharding import PartitionSpec as P

BF16 = jnp.bfloat16
F32 = jnp.float32
ND = 32
LANES = 128
C_STEP = 8
CUTS = (0, 384, 768, 1024)
ORDERS = ("xyz", "yzx", "zxy")
T_ORDER = ("y2", "x1", "x2")
FIRST = (1, 3)
SECOND = (3, 1)


def device_at(x, y, z, core):
    return (((y // 2) * 4 + x) * 2 + core) * 8 + z * 2 + y % 2


def flipped(move):
    pairs = []
    for y in range(4):
        for x in range(4):
            for z in range(4):
                for core in range(2):
                    to = dict(x=x, y=y, z=z, core=core)
                    if move == "core":
                        to["core"] = 1 - core
                    elif move == "y2h":
                        to["y"] = y ^ 2
                    else:
                        to[move[0]] ^= (FIRST if move[1] == "1" else SECOND)[core]
                    pairs.append((device_at(x, y, z, core), device_at(**to)))
    return pairs


def swap(value, move):
    return lax.ppermute(value, ("aa", "col"), flipped(move))


def grown(value, move):
    return jnp.concatenate([value, swap(value, move)], axis=0)


def split(value):
    high = value.astype(BF16)
    return high, (value - high.astype(F32)).astype(BF16)


def dot(a, b):
    return jnp.dot(a, b, preferred_element_type=F32)


def dot3(a_high, a_low, b_high, b_low):
    return dot(a_high, b_high) + (dot(a_high, b_low) + dot(a_low, b_high))


def position():
    aa, col = lax.axis_index("aa"), lax.axis_index("col")
    y = (aa // 8) * 2 + col % 2
    return (aa // 2) % 4, y, col // 2, aa % 2


def chosen(core, pair):
    return jnp.where(core == 0, pair[0], pair[1])


def bit(j, at):
    return (j >> at) & 1


def fit_rows(j, half, order, core, x, y, z):
    first, second = chosen(core, FIRST), chosen(core, SECOND)
    moved = {"z": bit(j, 0) * first, "y": bit(j, 1) * first, "x": bit(j, 2) * first}
    for at, dim in enumerate(order):
        flip = half if at == 2 else bit(j, 3 + at)
        moved[dim] = moved[dim] ^ (flip * second)
    x, y, z = x ^ moved["x"], y ^ moved["y"], z ^ moved["z"]
    return (((y // 2) * 4 + x) * 2 + core) * 128 + z * 32 + (y % 2) * 16


def amplitude_d(j, half, core, x, y):
    first, second = chosen(core, FIRST), chosen(core, SECOND)
    high = (y // 2) ^ bit(j, 0)
    x = x ^ (bit(j, 1) * first) ^ (half * second)
    return ((high * 4 + x) * 2 + core) * 2


def kernel(*refs, n_fit, n_amp, nt, a_size, k_size, b_size):
    where_ref, a_ref = refs[0], refs[1]
    fits = refs[2 : 2 + n_fit]
    amps = refs[2 + n_fit : 2 + n_fit + n_amp]
    r_ref, fh, fl, ah, al, xh, xl, th, tl, vs, ts = refs[2 + n_fit + n_amp :]
    step = pl.program_id(0)
    x, y, z, core = (where_ref[i] for i in range(4))
    c_size, columns = C_STEP, fh.shape[1]
    lane_tiles = nt // LANES

    @pl.when(step == 0)
    def _():
        for at, ref in enumerate(fits):
            part, half, other = at // 4, (at // 2) % 2, at % 2
            cols = slice(CUTS[part], CUTS[part + 1])
            owner = core if other == 0 else 1 - core

            def place(j, carry):
                rows = fit_rows(j, half, ORDERS[part], owner, x, y, z)
                rows = pl.ds(pl.multiple_of(rows, 16), 16)
                high, low = split(ref[j])
                fh[rows, cols] = high
                fl[rows, cols] = low
                return carry

            lax.fori_loop(0, 32, place, 0, unroll=4)
        r_ref[...] = jnp.zeros_like(r_ref)

    for i in range(0, a_size, 4):
        high, low = split(a_ref[i : i + 4].reshape(4 * c_size, a_ref.shape[2]))
        ah[i * c_size : (i + 4) * c_size, :] = high
        al[i * c_size : (i + 4) * c_size, :] = low
    for k in range(k_size):
        for at, ref in enumerate(amps):
            half, owner = at // 2, (core if at % 2 == 0 else 1 - core)
            for j in range(4):
                d = amplitude_d(jnp.int32(j), half, owner, x, y)
                for dl in range(2):
                    rows = pl.ds(pl.multiple_of((d + dl) * c_size, c_size), c_size)
                    for lt in range(ts.shape[1]):
                        ts[k, lt, rows, :] = ref[j, k, dl, :, lt * LANES : (lt + 1) * LANES]
        for c in range(c_size):
            for lt in range(ts.shape[1]):
                high, low = split(ts[k, lt, pl.ds(c, ND, stride=c_size), :])
                rows, lanes = slice(c * ND, (c + 1) * ND), slice(lt * LANES, (lt + 1) * LANES)
                th[k, rows, lanes] = high
                tl[k, rows, lanes] = low

    lane = lax.broadcasted_iota(jnp.int32, (a_size, LANES), 1)
    front, even = lane < 64, (lane // 32) % 2 == 0
    for n in range(columns // nt):
        cols = slice(n * nt, (n + 1) * nt)
        value = dot3(ah[...], al[...], fh[:, cols], fl[:, cols])
        for lt in range(lane_tiles):
            vs[n * lane_tiles + lt] = value[:, lt * LANES : (lt + 1) * LANES]
        for lt in range(lane_tiles):
            tile = n * lane_tiles + lt
            for cq in range(c_size // 4):
                q = [vs[tile, pl.ds(cq * 4 + j, a_size, stride=c_size), :] for j in range(4)]
                s = [
                    jnp.where(front, q[0], pltpu.roll(q[2], 64, 1)),
                    jnp.where(front, q[1], pltpu.roll(q[3], 64, 1)),
                    jnp.where(front, pltpu.roll(q[0], 64, 1), q[2]),
                    jnp.where(front, pltpu.roll(q[1], 64, 1), q[3]),
                ]
                w = [
                    jnp.where(even, s[0], pltpu.roll(s[1], 32, 1)),
                    jnp.where(even, pltpu.roll(s[0], 96, 1), s[1]),
                    jnp.where(even, s[2], pltpu.roll(s[3], 32, 1)),
                    jnp.where(even, pltpu.roll(s[2], 96, 1), s[3]),
                ]
                for b in range(4):
                    high, low = split(w[b])
                    row = (tile * 4 + b) * a_size
                    xh[row : row + a_size, cq * LANES : (cq + 1) * LANES] = high
                    xl[row : row + a_size, cq * LANES : (cq + 1) * LANES] = low
    for k in range(k_size):
        rows = slice(k * b_size * a_size, (k + 1) * b_size * a_size)
        value = dot3(xh[rows, :], xl[rows, :], th[k], tl[k])
        r_ref[:, k] += value.reshape(b_size, a_size, value.shape[1])


def contracted(where, fit_ac, fits, amps, nt=512):
    a_size, c_local, q_size = fit_ac.shape
    k_size, pairs = amps[0].shape[1], amps[0].shape[4]
    columns = CUTS[-1]
    b_size = columns // (k_size * ND)
    rows = a_size * C_STEP
    whole = lambda value: pl.BlockSpec(
        value.shape, lambda i, w: (0,) * value.ndim, pipeline_mode=pl.Buffered(1)
    )
    grid_spec = pltpu.PrefetchScalarGridSpec(
        num_scalar_prefetch=1,
        grid=(c_local // C_STEP,),
        in_specs=[pl.BlockSpec((a_size, C_STEP, q_size), lambda i, w: (0, i, 0))]
        + [whole(value) for value in fits]
        + [
            pl.BlockSpec((4, k_size, 2, C_STEP, pairs), lambda i, w: (0, 0, 0, i, 0))
            for _ in amps
        ],
        out_specs=pl.BlockSpec((b_size, k_size, a_size, pairs), lambda i, w: (0, 0, 0, 0)),
        scratch_shapes=[
            pltpu.VMEM((q_size, columns), BF16),
            pltpu.VMEM((q_size, columns), BF16),
            pltpu.VMEM((rows, q_size), BF16),
            pltpu.VMEM((rows, q_size), BF16),
            pltpu.VMEM((k_size * b_size * a_size, C_STEP * ND), BF16),
            pltpu.VMEM((k_size * b_size * a_size, C_STEP * ND), BF16),
            pltpu.VMEM((k_size, C_STEP * ND, pairs), BF16),
            pltpu.VMEM((k_size, C_STEP * ND, pairs), BF16),
            pltpu.VMEM((columns // LANES, rows, LANES), F32),
            pltpu.VMEM((k_size, pairs // LANES, ND * C_STEP, LANES), F32),
        ],
    )
    return pl.pallas_call(
        functools.partial(
            kernel, n_fit=len(fits), n_amp=len(amps), nt=nt, a_size=a_size, k_size=k_size, b_size=b_size
        ),
        grid_spec=grid_spec,
        out_shape=jax.ShapeDtypeStruct((b_size, k_size, a_size, pairs), F32),
        compiler_params=pltpu.CompilerParams(vmem_limit_bytes=58 << 20),
    )(where, fit_ac, *fits, *amps)


def gathered_fit(fit_bd):
    value = fit_bd[None]
    for move in ("z1", "y1", "x1"):
        value = grown(value, move)
    parts = [value[:, :, CUTS[i] : CUTS[i + 1]] for i in range(3)]
    for at in range(2):
        parts = [grown(part, order[at] + "2") for part, order in zip(parts, ORDERS)]
    arrived = [swap(part, order[2] + "2") for part, order in zip(parts, ORDERS)]
    near = [swap(part, "core") for part in parts]
    far = [swap(part, "core") for part in arrived]
    return [v for four in zip(parts, near, arrived, far) for v in four]


def gathered_amplitudes(amplitudes):
    value = amplitudes[None]
    value = grown(value, "y2h")
    value = grown(value, "x1")
    arrived = swap(value, "x2")
    return [value, swap(value, "core"), arrived, swap(arrived, "core")]


def shards(fit_ac, fit_bd, amplitudes):
    x, y, z, core = position()
    where = jnp.stack([x, y, z, core]).astype(jnp.int32)
    fits = gathered_fit(fit_bd)
    amps = gathered_amplitudes(amplitudes)
    partial = contracted(where, fit_ac, fits, amps)
    b_size, k_size, a_size, pairs = partial.shape
    peers = lax.axis_size("col")
    pieces = partial.reshape(peers, b_size // peers, k_size, a_size, pairs)
    pieces = lax.all_to_all(pieces, "col", 0, 0, tiled=True)
    return jnp.sum(pieces, axis=0).transpose(1, 0, 2, 3)


def solution(mesh):
    placed = (P("aa", "col", None), P(("aa", "col"), None), P(None, "aa", "col", None))
    return jax.shard_map(
        shards, mesh=mesh, in_specs=placed, out_specs=P(None, "col", "aa", None), check_vma=False
    )
```

time: 282 us -> 142 us (0.50)
  matrix products: 147 us -> 0 us
  Pallas kernels: 0 us -> 47.9 us
  waiting for transfers between devices: 72 us -> 31.1 us
  starting transfers between devices: 0.04 us -> 33.5 us
  blocking collectives: 36.8 us -> 21.6 us
  between operations: 13.4 us -> 0.17 us
  local copies, waits for them, and re-layouts: 11.8 us -> 1.02 us
  other arithmetic: 0.45 us -> 6.23 us
    dot_general x2 -> x0, matrix products: 147 us -> none  [the longest x1 131 us: contract_rows(): jnp.dot(fitting_rows, piece, precision=lax.Precision.HIGHEST, preferred_e...]
    all_gather x2 -> x0, waiting for transfers between devices: 71.3 us -> none  [the longest x1 71.2 us: shards(): lax.all_gather(grouped, 'aa', axis=0, tiled=True)]
    pallas_call x0 -> x1, Pallas kernels: none -> 47.9 us  [contracted(): pl.pallas_call(functools.partial(kernel, n_fit=len(fits), n_amp=len(amps)...]
    ppermute x0 -> x23, starting transfers between devices: none -> 33.5 us  [swap(): return lax.ppermute(value, ('aa', 'col'), flipped(move))]
    ppermute x0 -> x23, waiting for transfers between devices: none -> 31.1 us  [swap(): return lax.ppermute(value, ('aa', 'col'), flipped(move))]
    all_to_all x2 -> x1, blocking collectives: 36.8 us -> 21.6 us  [shards(): pieces = lax.all_to_all(pieces, 'col', 0, 0, tiled=True)]
    dot_general x1 -> x0, local copies, waits for them, and re-layouts: 9.14 us -> none  [contract_rows(): jnp.dot(fitting_rows, piece, precision=lax.Precision.HIGHEST, preferred_e...]
    concatenate x0 -> x11, other arithmetic: none -> 4.83 us  [grown(): return jnp.concatenate([value, swap(value, move)], axis=0)]
  transfers between devices with their start and end apart: 2 -> 23, of which waited for: 1 -> 11; matrix products, arithmetic and copies ran while one was open for 50% -> 3% of each run, Pallas kernels for 0% -> 0%
where the time goes in v1:
time: 142 us; the launch traced here: 141 us
  Pallas kernels  47.9 us (34%)
  starting transfers between devices  33.5 us (24%)
  waiting for transfers between devices  31.1 us (22%)
  blocking collectives  21.6 us (15%)
  other arithmetic  6.23 us (4%)
    pallas_call x1, Pallas kernels, contracted(): pl.pallas_call(functools.partial(kernel, n_fit=len(fits), n_amp=len(amps)...  47.9 us
    ppermute x23, starting transfers between devices, swap(): return lax.ppermute(value, ('aa', 'col'), flipped(move))  33.5 us
    ppermute x23, waiting for transfers between devices, swap(): return lax.ppermute(value, ('aa', 'col'), flipped(move))  31.1 us
    all_to_all x1, blocking collectives, shards(): pieces = lax.all_to_all(pieces, 'col', 0, 0, tiled=True)  21.6 us
    concatenate x11, other arithmetic, grown(): return jnp.concatenate([value, swap(value, move)], axis=0)  4.83 us
  transfers between devices with their start and end apart: 23, of which 11 were waited for; matrix products, arithmetic and copies ran while one was open for 3% of the time, Pallas kernels for 0%

profile of v1, /device:TPU:0, one launch (start us, length us, event | category | flops | bytes accessed | tf_op | source)
XLA Modules:
  0.0 141.4 jit_solution(1526482577454707109)
XLA Ops:
  0.0 2.0 %collective-permute-start = (f32[1,16,1024]{2,1,0:T(8,128)}, f32[1,16,1024]{2,1,0:T(8,128)S(1)}, u32[]{:S(2)}, u32[]{:S(2)}) collective-permute-start(f32[1,16,1024]{2,1,0:T(8,128)} %bitcast.9), channel_id=1, source_target_pairs={{0,2},{8,14},{2,0},{10,12},{4,6},{12,10},{6,4},{14,8},{16,18},{24,... | collective-permute-start | bytes 196616 | tf_op jit(solution)/shard_map/ppermute | solution.py:44
  2.0 2.5 %collective-permute-done = f32[1,16,1024]{2,1,0:T(8,128)S(1)} collective-permute-done((f32[1,16,1024]{2,1,0:T(8,128)}, f32[1,16,1024]{2,1,0:T(8,128)S(1)}, u32[]{:S(2)}, u32[]{:S(2)}) %collective-permute-start) | collective-permute-done | bytes 65568 | tf_op jit(solution)/shard_map/ppermute | solution.py:44
  4.5 0.9 pad_maximum_fusion.11
  5.3 1.7 %collective-permute-start.1 = (f32[2,16,1024]{2,1,0:T(8,128)S(1)}, f32[2,16,1024]{2,1,0:T(8,128)S(1)}, u32[]{:S(2)}, u32[]{:S(2)}) collective-permute-start(f32[2,16,1024]{2,1,0:T(8,128)S(1)} %pad_maximum_fusion.11), channel_id=1, source_target_pairs={{0,1},{8,73},{2,3},{10,75},{4,5},{12,77},{6,7},{14,79},{16,17},{24... | collective-permute-start | bytes 393224 | tf_op jit(solution)/shard_map/ppermute | solution.py:44
  7.1 3.3 %collective-permute-done.1 = f32[2,16,1024]{2,1,0:T(8,128)S(1)} collective-permute-done((f32[2,16,1024]{2,1,0:T(8,128)S(1)}, f32[2,16,1024]{2,1,0:T(8,128)S(1)}, u32[]{:S(2)}, u32[]{:S(2)}) %collective-permute-start.1) | collective-permute-done | bytes 131104 | tf_op jit(solution)/shard_map/ppermute | solution.py:44
  10.4 0.9 pad_maximum_fusion.8
  11.2 1.7 %collective-permute-start.2 = (f32[4,16,1024]{2,1,0:T(8,128)S(1)}, f32[4,16,1024]{2,1,0:T(8,128)S(1)}, u32[]{:S(2)}, u32[]{:S(2)}) collective-permute-start(f32[4,16,1024]{2,1,0:T(8,128)S(1)} %pad_maximum_fusion.8), channel_id=1, source_target_pairs={{0,16},{8,56},{2,18},{10,58},{4,20},{12,60},{6,22},{14,62},{16,0},... | collective-permute-start | bytes 786440 | tf_op jit(solution)/shard_map/ppermute | solution.py:44
  12.9 3.2 %collective-permute-start.18 = (f32[1,2,2,64,256]{4,3,2,1,0:T(8,128)}, f32[1,2,2,64,256]{4,3,2,1,0:T(8,128)S(1)}, u32[]{:S(2)}, u32[]{:S(2)}) collective-permute-start(f32[1,2,2,64,256]{4,3,2,1,0:T(8,128)} %bitcast.14), channel_id=1, source_target_pairs={{0,64},{8,72},{2,66},{10,74},{4,68},{12,76},{6,70},{14,78},{16,80}... | collective-permute-start | bytes 786440 | tf_op jit(solution)/shard_map/ppermute | solution.py:44
  16.1 1.6 %collective-permute-done.2 = f32[4,16,1024]{2,1,0:T(8,128)S(1)} collective-permute-done((f32[4,16,1024]{2,1,0:T(8,128)S(1)}, f32[4,16,1024]{2,1,0:T(8,128)S(1)}, u32[]{:S(2)}, u32[]{:S(2)}) %collective-permute-start.2) | collective-permute-done | bytes 262176 | tf_op jit(solution)/shard_map/ppermute | solution.py:44
  17.7 0.7 pad_maximum_fusion.10
  18.4 4.2 %collective-permute-start.13 = (f32[8,16,256]{2,1,0:T(8,128)S(1)}, f32[8,16,256]{2,1,0:T(8,128)S(1)}, u32[]{:S(2)}, u32[]{:S(2)}) collective-permute-start(f32[8,16,256]{2,1,0:T(8,128)S(1)} %pad_maximum_fusion.10), channel_id=1, source_target_pairs={{0,6},{8,10},{2,4},{10,8},{4,2},{12,14},{6,0},{14,12},{16,22},{24,... | collective-permute-start | bytes 393224 | tf_op jit(solution)/shard_map/ppermute | solution.py:44
  22.6 0.9 pad_maximum_fusion.3
  23.5 3.1 %collective-permute-start.8 = (f32[8,16,384]{2,1,0:T(8,128)S(1)}, f32[8,16,384]{2,1,0:T(8,128)S(1)}, u32[]{:S(2)}, u32[]{:S(2)}) collective-permute-start(f32[8,16,384]{2,1,0:T(8,128)S(1)} %get-tuple-element.5), channel_id=1, source_target_pairs={{0,65},{8,9},{2,67},{10,11},{4,69},{12,13},{6,71},{14,15},{16,81},... | collective-permute-start | bytes 589832 | tf_op jit(solution)/shard_map/ppermute | solution.py:44
  26.6 1.0 pad_maximum_fusion.5
  27.6 1.6 %collective-permute-start.19 = (f32[2,2,2,64,256]{4,3,2,1,0:T(8,128)S(1)}, f32[2,2,2,64,256]{4,3,2,1,0:T(8,128)S(1)}, u32[]{:S(2)}, u32[]{:S(2)}) collective-permute-start(f32[2,2,2,64,256]{4,3,2,1,0:T(8,128)S(1)} %pad_maximum_fusion.5), channel_id=1, source_target_pairs={{0,16},{8,56},{2,18},{10,58},{4,20},{12,60},{6,22},{14,62},{16,0},... | collective-permute-start | bytes 1572872 | tf_op jit(solution)/shard_map/ppermute | solution.py:44
  29.2 2.1 %collective-permute-start.3 = (f32[8,16,384]{2,1,0:T(8,128)S(1)}, f32[8,16,384]{2,1,0:T(8,128)S(1)}, u32[]{:S(2)}, u32[]{:S(2)}) collective-permute-start(f32[8,16,384]{2,1,0:T(8,128)S(1)} %get-tuple-element.6), channel_id=1, source_target_pairs={{0,48},{8,24},{2,50},{10,26},{4,52},{12,28},{6,54},{14,30},{16,32}... | collective-permute-start | bytes 589832 | tf_op jit(solution)/shard_map/ppermute | solution.py:44
  31.3 1.2 collective-permute-start.14
  32.5 0.0 collective-permute-done.8
  32.6 0.1 collective-permute-start.9
  32.7 3.5 %collective-permute-done.3 = f32[8,16,384]{2,1,0:T(8,128)S(1)} collective-permute-done((f32[8,16,384]{2,1,0:T(8,128)S(1)}, f32[8,16,384]{2,1,0:T(8,128)S(1)}, u32[]{:S(2)}, u32[]{:S(2)}) %collective-permute-start.3) | collective-permute-done | bytes 196640 | tf_op jit(solution)/shard_map/ppermute | solution.py:44
  36.2 2.3 %collective-permute-start.4 = (f32[16,16,384]{2,1,0:T(8,128)S(1)}, f32[16,16,384]{2,1,0:T(8,128)S(1)}, u32[]{:S(2)}, u32[]{:S(2)}) collective-permute-start(f32[16,16,384]{2,1,0:T(8,128)S(1)} %pad_maximum_fusion.6), channel_id=1, source_target_pairs={{0,65},{8,9},{2,67},{10,11},{4,69},{12,13},{6,71},{14,15},{16,81},... | collective-permute-start | bytes 1179656 | tf_op jit(solution)/shard_map/ppermute | solution.py:44
  38.6 0.4 collective-permute-done.14
  39.1 3.1 %collective-permute-start.16 = (f32[32,16,256]{2,1,0:T(8,128)S(1)}, f32[32,16,256]{2,1,0:T(8,128)}, u32[]{:S(2)}, u32[]{:S(2)}) collective-permute-start(f32[32,16,256]{2,1,0:T(8,128)S(1)} %pad_maximum_fusion.4.refs_10_), channel_id=1, source_target_pairs={{0,65},{8,9},{2,67},{10,11},{4,69},{12,13},{6,71},{14,15},{16,81},... | collective-permute-start | bytes 1572872 | tf_op jit(solution)/shard_map/ppermute | solution.py:44
  42.2 0.0 collective-permute-done.19
  42.2 1.0 pad_maximum_fusion.refs_14_
  43.2 1.5 %collective-permute-start.21 = (f32[4,2,2,64,256]{4,3,2,1,0:T(8,128)S(1)}, f32[4,2,2,64,256]{4,3,2,1,0:T(8,128)}, u32[]{:S(2)}, u32[]{:S(2)}) collective-permute-start(f32[4,2,2,64,256]{4,3,2,1,0:T(8,128)S(1)} %pad_maximum_fusion.refs_14_), channel_id=1, source_target_pairs={{0,48},{8,24},{2,50},{10,26},{4,52},{12,28},{6,54},{14,30},{16,32}... | collective-permute-start | bytes 3145736 | tf_op jit(solution)/shard_map/ppermute | solution.py:44
  44.7 0.6 collective-permute-done.4
  45.3 0.1 pad_maximum_fusion.1.refs_2_
  45.4 2.6 %collective-permute-start.6 = (f32[32,16,384]{2,1,0:T(8,128)S(1)}, f32[32,16,384]{2,1,0:T(8,128)}, u32[]{:S(2)}, u32[]{:S(2)}) collective-permute-start(f32[32,16,384]{2,1,0:T(8,128)S(1)} %pad_maximum_fusion.1.refs_2_), channel_id=1, source_target_pairs={{0,6},{8,10},{2,4},{10,8},{4,2},{12,14},{6,0},{14,12},{16,22},{24,... | collective-permute-start | bytes 2359304 | tf_op jit(solution)/shard_map/ppermute | solution.py:44
  48.0 0.1 pad_maximum_fusion.2.refs_6_
  48.1 2.9 %collective-permute-done.16.refs_12_ = f32[32,16,256]{2,1,0:T(8,128)} collective-permute-done((f32[32,16,256]{2,1,0:T(8,128)S(1)}, f32[32,16,256]{2,1,0:T(8,128)}, u32[]{:S(2)}, u32[]{:S(2)}) %collective-permute-start.16) | collective-permute-done | bytes 524320 | tf_op jit(solution)/shard_map/ppermute | solution.py:44
  51.0 2.0 %collective-permute-start.11 = (f32[32,16,384]{2,1,0:T(8,128)S(1)}, f32[32,16,384]{2,1,0:T(8,128)}, u32[]{:S(2)}, u32[]{:S(2)}) collective-permute-start(f32[32,16,384]{2,1,0:T(8,128)S(1)} %pad_maximum_fusion.2.refs_6_), channel_id=1, source_target_pairs={{0,48},{8,24},{2,50},{10,26},{4,52},{12,28},{6,54},{14,30},{16,32}... | collective-permute-start | bytes 2359304 | tf_op jit(solution)/shard_map/ppermute | solution.py:44
  53.0 0.0 collective-permute-done.15.refs_11_
  53.0 0.0 collective-permute-start.10
  53.0 5.7 %collective-permute-done.6.refs_4_ = f32[32,16,384]{2,1,0:T(8,128)} collective-permute-done((f32[32,16,384]{2,1,0:T(8,128)S(1)}, f32[32,16,384]{2,1,0:T(8,128)}, u32[]{:S(2)}, u32[]{:S(2)}) %collective-permute-start.6) | collective-permute-done | bytes 786464 | tf_op jit(solution)/shard_map/ppermute | solution.py:44
  58.8 0.7 collective-permute-done.21.refs_16_
  59.4 0.0 collective-permute-start.22
  59.4 0.0 collective-permute-done.5.refs_3_
  59.4 0.5 collective-permute-start.7
  59.9 7.9 %collective-permute-done.11.refs_8_ = f32[32,16,384]{2,1,0:T(8,128)} collective-permute-done((f32[32,16,384]{2,1,0:T(8,128)S(1)}, f32[32,16,384]{2,1,0:T(8,128)}, u32[]{:S(2)}, u32[]{:S(2)}) %collective-permute-start.11) | collective-permute-done | bytes 786464 | tf_op jit(solution)/shard_map/ppermute | solution.py:44
  67.9 0.6 collective-permute-start.17
  68.4 0.3 copy-done.5
  68.7 0.6 pad_add_fusion.refs_0_
  69.3 1.9 %collective-permute-done.17.refs_13_ = f32[32,16,256]{2,1,0:T(8,128)} collective-permute-done((f32[32,16,256]{2,1,0:T(8,128)}, f32[32,16,256]{2,1,0:T(8,128)}, u32[]{:S(2)}, u32[]{:S(2)}) %collective-permute-start.17) | collective-permute-done | bytes 524320 | tf_op jit(solution)/shard_map/ppermute | solution.py:44
  71.3 47.9 %shard_map.37 = f32[16,2,32,256]{3,2,1,0:T(8,128)} custom-call(s32[4]{0:T(128)} %pad_add_fusion.refs_0_, f32[32,64,2048]{2,1,0:T(8,128)} %refs_1_.1, f32[32,16,384]{2,1,0:T(8,128)} %copy-done.1, f32[32,16,384]{2,1,0:T(8,128)} %copy-done.4, f32[32,16,384]{2,1,0:T(8,128)} %collective-permute-done.6.refs_4_, f32[32,16,384]{2,1,0:T(8,128)} %collective-permute-done.7.refs_5_, ...), custom_call_target="tpu_custom_call" | custom-call | tf_op jit(solution)/shard_map/pallas_call | solution.py:209
  119.1 21.6 %all_to_all.5 = f32[8,2,2,32,256]{4,3,2,1,0:T(8,128)S(1)} all-to-all(f32[8,2,2,32,256]{4,3,2,1,0:T(8,128)} %bitcast.8), channel_id=1, replica_groups=mesh['aa'=16,'col'=8] {'col'}, dimensions={0} | all-to-all | bytes 2097152 | tf_op jit(solution)/shard_map/all_to_all | solution.py:249
  140.7 0.1 reduce_sum.9
  140.8 0.7 copy.4
  (30 shorter events, 0.2 us)
Async XLA Ops:
  0.0 4.5 %collective-permute-start = (f32[1,16,1024]{2,1,0:T(8,128)}, f32[1,16,1024]{2,1,0:T(8,128)S(1)}, u32[]{:S(2)}, u32[]{:S(2)}) collective-permute-start(f32[1,16,1024]{2,1,0:T(8,128)} %bitcast.9), channel_id=1, source_target_pairs={{0,2},{8,14},{2,0},{10,12},{4,6},{12,10},{6,4},{14,8},{16,18},{24,... | collective-permute-start | bytes 196616 | tf_op jit(solution)/shard_map/ppermute | solution.py:44
  5.3 5.0 %collective-permute-start.1 = (f32[2,16,1024]{2,1,0:T(8,128)S(1)}, f32[2,16,1024]{2,1,0:T(8,128)S(1)}, u32[]{:S(2)}, u32[]{:S(2)}) collective-permute-start(f32[2,16,1024]{2,1,0:T(8,128)S(1)} %pad_maximum_fusion.11), channel_id=1, source_target_pairs={{0,1},{8,73},{2,3},{10,75},{4,5},{12,77},{6,7},{14,79},{16,17},{24... | collective-permute-start | bytes 393224 | tf_op jit(solution)/shard_map/ppermute | solution.py:44
  11.2 6.5 %collective-permute-start.2 = (f32[4,16,1024]{2,1,0:T(8,128)S(1)}, f32[4,16,1024]{2,1,0:T(8,128)S(1)}, u32[]{:S(2)}, u32[]{:S(2)}) collective-permute-start(f32[4,16,1024]{2,1,0:T(8,128)S(1)} %pad_maximum_fusion.8), channel_id=1, source_target_pairs={{0,16},{8,56},{2,18},{10,58},{4,20},{12,60},{6,22},{14,62},{16,0},... | collective-permute-start | bytes 786440 | tf_op jit(solution)/shard_map/ppermute | solution.py:44
  12.9 13.8 %collective-permute-start.18 = (f32[1,2,2,64,256]{4,3,2,1,0:T(8,128)}, f32[1,2,2,64,256]{4,3,2,1,0:T(8,128)S(1)}, u32[]{:S(2)}, u32[]{:S(2)}) collective-permute-start(f32[1,2,2,64,256]{4,3,2,1,0:T(8,128)} %bitcast.14), channel_id=1, source_target_pairs={{0,64},{8,72},{2,66},{10,74},{4,68},{12,76},{6,70},{14,78},{16,80}... | collective-permute-start | bytes 786440 | tf_op jit(solution)/shard_map/ppermute | solution.py:44
  18.4 12.9 %collective-permute-start.13 = (f32[8,16,256]{2,1,0:T(8,128)S(1)}, f32[8,16,256]{2,1,0:T(8,128)S(1)}, u32[]{:S(2)}, u32[]{:S(2)}) collective-permute-start(f32[8,16,256]{2,1,0:T(8,128)S(1)} %pad_maximum_fusion.10), channel_id=1, source_target_pairs={{0,6},{8,10},{2,4},{10,8},{4,2},{12,14},{6,0},{14,12},{16,22},{24,... | collective-permute-start | bytes 393224 | tf_op jit(solution)/shard_map/ppermute | solution.py:44
  23.5 9.0 %collective-permute-start.8 = (f32[8,16,384]{2,1,0:T(8,128)S(1)}, f32[8,16,384]{2,1,0:T(8,128)S(1)}, u32[]{:S(2)}, u32[]{:S(2)}) collective-permute-start(f32[8,16,384]{2,1,0:T(8,128)S(1)} %get-tuple-element.5), channel_id=1, source_target_pairs={{0,65},{8,9},{2,67},{10,11},{4,69},{12,13},{6,71},{14,15},{16,81},... | collective-permute-start | bytes 589832 | tf_op jit(solution)/shard_map/ppermute | solution.py:44
  27.6 14.5 %collective-permute-start.19 = (f32[2,2,2,64,256]{4,3,2,1,0:T(8,128)S(1)}, f32[2,2,2,64,256]{4,3,2,1,0:T(8,128)S(1)}, u32[]{:S(2)}, u32[]{:S(2)}) collective-permute-start(f32[2,2,2,64,256]{4,3,2,1,0:T(8,128)S(1)} %pad_maximum_fusion.5), channel_id=1, source_target_pairs={{0,16},{8,56},{2,18},{10,58},{4,20},{12,60},{6,22},{14,62},{16,0},... | collective-permute-start | bytes 1572872 | tf_op jit(solution)/shard_map/ppermute | solution.py:44
  29.2 7.0 %collective-permute-start.3 = (f32[8,16,384]{2,1,0:T(8,128)S(1)}, f32[8,16,384]{2,1,0:T(8,128)S(1)}, u32[]{:S(2)}, u32[]{:S(2)}) collective-permute-start(f32[8,16,384]{2,1,0:T(8,128)S(1)} %get-tuple-element.6), channel_id=1, source_target_pairs={{0,48},{8,24},{2,50},{10,26},{4,52},{12,28},{6,54},{14,30},{16,32}... | collective-permute-start | bytes 589832 | tf_op jit(solution)/shard_map/ppermute | solution.py:44
  31.3 7.7 %collective-permute-start.14 = (f32[16,16,256]{2,1,0:T(8,128)S(1)}, f32[16,16,256]{2,1,0:T(8,128)S(1)}, u32[]{:S(2)}, u32[]{:S(2)}) collective-permute-start(f32[16,16,256]{2,1,0:T(8,128)S(1)} %pad_maximum_fusion.9), channel_id=1, source_target_pairs={{0,48},{8,24},{2,50},{10,26},{4,52},{12,28},{6,54},{14,30},{16,32}... | collective-permute-start | bytes 786440 | tf_op jit(solution)/shard_map/ppermute | solution.py:44
  32.6 15.4 %collective-permute-start.9 = (f32[16,16,384]{2,1,0:T(8,128)S(1)}, f32[16,16,384]{2,1,0:T(8,128)S(1)}, u32[]{:S(2)}, u32[]{:S(2)}) collective-permute-start(f32[16,16,384]{2,1,0:T(8,128)S(1)} %pad_maximum_fusion.7), channel_id=1, source_target_pairs={{0,6},{8,10},{2,4},{10,8},{4,2},{12,14},{6,0},{14,12},{16,22},{24,... | collective-permute-start | bytes 1179656 | tf_op jit(solution)/shard_map/ppermute | solution.py:44
  36.2 9.1 %collective-permute-start.4 = (f32[16,16,384]{2,1,0:T(8,128)S(1)}, f32[16,16,384]{2,1,0:T(8,128)S(1)}, u32[]{:S(2)}, u32[]{:S(2)}) collective-permute-start(f32[16,16,384]{2,1,0:T(8,128)S(1)} %pad_maximum_fusion.6), channel_id=1, source_target_pairs={{0,65},{8,9},{2,67},{10,11},{4,69},{12,13},{6,71},{14,15},{16,81},... | collective-permute-start | bytes 1179656 | tf_op jit(solution)/shard_map/ppermute | solution.py:44
  39.1 32.2 %copy-start.3 = (f32[32,16,256]{2,1,0:T(8,128)}, f32[32,16,256]{2,1,0:T(8,128)S(1)}, u32[]{:S(2)}) copy-start(f32[32,16,256]{2,1,0:T(8,128)S(1)} %pad_maximum_fusion.4.refs_10_) | copy-start | bytes 1572868
  39.1 12.0 %collective-permute-start.16 = (f32[32,16,256]{2,1,0:T(8,128)S(1)}, f32[32,16,256]{2,1,0:T(8,128)}, u32[]{:S(2)}, u32[]{:S(2)}) collective-permute-start(f32[32,16,256]{2,1,0:T(8,128)S(1)} %pad_maximum_fusion.4.refs_10_), channel_id=1, source_target_pairs={{0,65},{8,9},{2,67},{10,11},{4,69},{12,13},{6,71},{14,15},{16,81},... | collective-permute-start | bytes 1572872 | tf_op jit(solution)/shard_map/ppermute | solution.py:44
  43.2 28.0 %copy-start = (f32[4,2,2,64,256]{4,3,2,1,0:T(8,128)}, f32[4,2,2,64,256]{4,3,2,1,0:T(8,128)S(1)}, u32[]{:S(2)}) copy-start(f32[4,2,2,64,256]{4,3,2,1,0:T(8,128)S(1)} %pad_maximum_fusion.refs_14_) | copy-start | bytes 3145732
  43.2 16.2 %collective-permute-start.21 = (f32[4,2,2,64,256]{4,3,2,1,0:T(8,128)S(1)}, f32[4,2,2,64,256]{4,3,2,1,0:T(8,128)}, u32[]{:S(2)}, u32[]{:S(2)}) collective-permute-start(f32[4,2,2,64,256]{4,3,2,1,0:T(8,128)S(1)} %pad_maximum_fusion.refs_14_), channel_id=1, source_target_pairs={{0,48},{8,24},{2,50},{10,26},{4,52},{12,28},{6,54},{14,30},{16,32}... | collective-permute-start | bytes 3145736 | tf_op jit(solution)/shard_map/ppermute | solution.py:44
  44.7 8.3 %collective-permute-start.15 = (f32[32,16,256]{2,1,0:T(8,128)S(1)}, f32[32,16,256]{2,1,0:T(8,128)S(1)}, u32[]{:S(2)}, u32[]{:S(2)}) collective-permute-start(f32[32,16,256]{2,1,0:T(8,128)S(1)} %pad_maximum_fusion.4.refs_10_), channel_id=1, source_target_pairs={{0,8},{8,0},{2,10},{10,2},{4,12},{12,4},{6,14},{14,6},{16,24},{24,... | collective-permute-start | bytes 1572872 | tf_op jit(solution)/shard_map/ppermute | solution.py:44
  45.4 25.9 %copy-start.1 = (f32[32,16,384]{2,1,0:T(8,128)}, f32[32,16,384]{2,1,0:T(8,128)S(1)}, u32[]{:S(2)}) copy-start(f32[32,16,384]{2,1,0:T(8,128)S(1)} %pad_maximum_fusion.1.refs_2_) | copy-start | bytes 2359300
  45.4 13.4 %collective-permute-start.6 = (f32[32,16,384]{2,1,0:T(8,128)S(1)}, f32[32,16,384]{2,1,0:T(8,128)}, u32[]{:S(2)}, u32[]{:S(2)}) collective-permute-start(f32[32,16,384]{2,1,0:T(8,128)S(1)} %pad_maximum_fusion.1.refs_2_), channel_id=1, source_target_pairs={{0,6},{8,10},{2,4},{10,8},{4,2},{12,14},{6,0},{14,12},{16,22},{24,... | collective-permute-start | bytes 2359304 | tf_op jit(solution)/shard_map/ppermute | solution.py:44
  48.0 11.4 %collective-permute-start.5 = (f32[32,16,384]{2,1,0:T(8,128)S(1)}, f32[32,16,384]{2,1,0:T(8,128)S(1)}, u32[]{:S(2)}, u32[]{:S(2)}) collective-permute-start(f32[32,16,384]{2,1,0:T(8,128)S(1)} %pad_maximum_fusion.1.refs_2_), channel_id=1, source_target_pairs={{0,8},{8,0},{2,10},{10,2},{4,12},{12,4},{6,14},{14,6},{16,24},{24,... | collective-permute-start | bytes 2359304 | tf_op jit(solution)/shard_map/ppermute | solution.py:44
  48.1 23.2 %copy-start.2 = (f32[32,16,384]{2,1,0:T(8,128)}, f32[32,16,384]{2,1,0:T(8,128)S(1)}, u32[]{:S(2)}) copy-start(f32[32,16,384]{2,1,0:T(8,128)S(1)} %pad_maximum_fusion.2.refs_6_) | copy-start | bytes 2359300
  51.0 16.8 %collective-permute-start.11 = (f32[32,16,384]{2,1,0:T(8,128)S(1)}, f32[32,16,384]{2,1,0:T(8,128)}, u32[]{:S(2)}, u32[]{:S(2)}) collective-permute-start(f32[32,16,384]{2,1,0:T(8,128)S(1)} %pad_maximum_fusion.2.refs_6_), channel_id=1, source_target_pairs={{0,48},{8,24},{2,50},{10,26},{4,52},{12,28},{6,54},{14,30},{16,32}... | collective-permute-start | bytes 2359304 | tf_op jit(solution)/shard_map/ppermute | solution.py:44
  53.0 15.4 %copy-start.6 = (f32[32,16,256]{2,1,0:T(8,128)}, f32[32,16,256]{2,1,0:T(8,128)S(1)}, u32[]{:S(2)}) copy-start(f32[32,16,256]{2,1,0:T(8,128)S(1)} %collective-permute-done.15.refs_11_) | copy-start | bytes 1572868
  53.0 14.8 %collective-permute-start.10 = (f32[32,16,384]{2,1,0:T(8,128)S(1)}, f32[32,16,384]{2,1,0:T(8,128)S(1)}, u32[]{:S(2)}, u32[]{:S(2)}) collective-permute-start(f32[32,16,384]{2,1,0:T(8,128)S(1)} %pad_maximum_fusion.2.refs_6_), channel_id=1, source_target_pairs={{0,8},{8,0},{2,10},{10,2},{4,12},{12,4},{6,14},{14,6},{16,24},{24,... | collective-permute-start | bytes 2359304 | tf_op jit(solution)/shard_map/ppermute | solution.py:44
  58.8 10.6 %collective-permute-start.20 = (f32[4,2,2,64,256]{4,3,2,1,0:T(8,128)S(1)}, f32[4,2,2,64,256]{4,3,2,1,0:T(8,128)}, u32[]{:S(2)}, u32[]{:S(2)}) collective-permute-start(f32[4,2,2,64,256]{4,3,2,1,0:T(8,128)S(1)} %pad_maximum_fusion.refs_14_), channel_id=1, source_target_pairs={{0,8},{8,0},{2,10},{10,2},{4,12},{12,4},{6,14},{14,6},{16,24},{24,... | collective-permute-start | bytes 3145736 | tf_op jit(solution)/shard_map/ppermute | solution.py:44
  59.4 11.8 %collective-permute-start.22 = (f32[4,2,2,64,256]{4,3,2,1,0:T(8,128)}, f32[4,2,2,64,256]{4,3,2,1,0:T(8,128)}, u32[]{:S(2)}, u32[]{:S(2)}) collective-permute-start(f32[4,2,2,64,256]{4,3,2,1,0:T(8,128)} %collective-permute-done.21.refs_16_), channel_id=1, source_target_pairs={{0,8},{8,0},{2,10},{10,2},{4,12},{12,4},{6,14},{14,6},{16,24},{24,... | collective-permute-start | bytes 3145736 | tf_op jit(solution)/shard_map/ppermute | solution.py:44
  59.4 8.4 %copy-start.4 = (f32[32,16,384]{2,1,0:T(8,128)}, f32[32,16,384]{2,1,0:T(8,128)S(1)}, u32[]{:S(2)}) copy-start(f32[32,16,384]{2,1,0:T(8,128)S(1)} %collective-permute-done.5.refs_3_) | copy-start | bytes 2359300
  59.4 11.8 %collective-permute-start.7 = (f32[32,16,384]{2,1,0:T(8,128)}, f32[32,16,384]{2,1,0:T(8,128)}, u32[]{:S(2)}, u32[]{:S(2)}) collective-permute-start(f32[32,16,384]{2,1,0:T(8,128)} %collective-permute-done.6.refs_4_), channel_id=1, source_target_pairs={{0,8},{8,0},{2,10},{10,2},{4,12},{12,4},{6,14},{14,6},{16,24},{24,... | collective-permute-start | bytes 2359304 | tf_op jit(solution)/shard_map/ppermute | solution.py:44
  67.8 3.4 %collective-permute-start.12 = (f32[32,16,384]{2,1,0:T(8,128)}, f32[32,16,384]{2,1,0:T(8,128)}, u32[]{:S(2)}, u32[]{:S(2)}) collective-permute-start(f32[32,16,384]{2,1,0:T(8,128)} %collective-permute-done.11.refs_8_), channel_id=1, source_target_pairs={{0,8},{8,0},{2,10},{10,2},{4,12},{12,4},{6,14},{14,6},{16,24},{24,... | collective-permute-start | bytes 2359304 | tf_op jit(solution)/shard_map/ppermute | solution.py:44
  67.9 0.9 copy-start.5
  67.9 3.4 %collective-permute-start.17 = (f32[32,16,256]{2,1,0:T(8,128)}, f32[32,16,256]{2,1,0:T(8,128)}, u32[]{:S(2)}, u32[]{:S(2)}) collective-permute-start(f32[32,16,256]{2,1,0:T(8,128)} %collective-permute-done.16.refs_12_), channel_id=1, source_target_pairs={{0,8},{8,0},{2,10},{10,2},{4,12},{12,4},{6,14},{14,6},{16,24},{24,... | collective-permute-start | bytes 1572872 | tf_op jit(solution)/shard_map/ppermute | solution.py:44

commit v2 on v1

--- a/solution.py
+++ b/solution.py
@@ -12,6 +12,11 @@
 ND = 32
 LANES = 128
 C_STEP = 8
+N_STEP = 256
+F8 = jnp.float8_e5m2
+F_HIGH, F_LOW = 2.0**12, 2.0**21
+A_HIGH, A_LOW = 2.0**17, 2.0**26
+UNSCALE = 2.0**-38
 CUTS = (0, 384, 768, 1024)
 ORDERS = ("xyz", "yzx", "zxy")
 T_ORDER = ("y2", "x1", "x2")
@@ -75,16 +80,6 @@
     return (j >> at) & 1
 
 
-def fit_rows(j, half, order, core, x, y, z):
-    first, second = chosen(core, FIRST), chosen(core, SECOND)
-    moved = {"z": bit(j, 0) * first, "y": bit(j, 1) * first, "x": bit(j, 2) * first}
-    for at, dim in enumerate(order):
-        flip = half if at == 2 else bit(j, 3 + at)
-        moved[dim] = moved[dim] ^ (flip * second)
-    x, y, z = x ^ moved["x"], y ^ moved["y"], z ^ moved["z"]
-    return (((y // 2) * 4 + x) * 2 + core) * 128 + z * 32 + (y % 2) * 16
-
-
 def amplitude_d(j, half, core, x, y):
     first, second = chosen(core, FIRST), chosen(core, SECOND)
     high = (y // 2) ^ bit(j, 0)
@@ -92,39 +87,79 @@
     return ((high * 4 + x) * 2 + core) * 2
 
 
-def kernel(*refs, n_fit, n_amp, nt, a_size, k_size, b_size):
+def kernel(*refs, n_fit, n_amp, a_size, k_size, b_size):
     where_ref, a_ref = refs[0], refs[1]
     fits = refs[2 : 2 + n_fit]
     amps = refs[2 + n_fit : 2 + n_fit + n_amp]
-    r_ref, fh, fl, ah, al, xh, xl, th, tl, vs, ts = refs[2 + n_fit + n_amp :]
+    r_ref, fh, fl, f8, ah, a8, xh, xl, th, tl, vs, ts = refs[2 + n_fit + n_amp :]
     step = pl.program_id(0)
+    last = pl.num_programs(0) - 1
     x, y, z, core = (where_ref[i] for i in range(4))
-    c_size, columns = C_STEP, fh.shape[1]
-    lane_tiles = nt // LANES
+    c_size, (q_size, columns) = C_STEP, fh.shape
+    pairs = th.shape[2]
 
     @pl.when(step == 0)
     def _():
-        for at, ref in enumerate(fits):
-            part, half, other = at // 4, (at // 2) % 2, at % 2
-            cols = slice(CUTS[part], CUTS[part + 1])
+        for other in range(2):
             owner = core if other == 0 else 1 - core
-
-            def place(j, carry):
-                rows = fit_rows(j, half, ORDERS[part], owner, x, y, z)
-                rows = pl.ds(pl.multiple_of(rows, 16), 16)
-                high, low = split(ref[j])
-                fh[rows, cols] = high
-                fl[rows, cols] = low
-                return carry
-
-            lax.fori_loop(0, 32, place, 0, unroll=4)
+            first, second = chosen(owner, FIRST), chosen(owner, SECOND)
+            moves = [[0, second], [first, first ^ second]]
+            at_x = [[(x ^ m) * 256 + owner * 128 for m in row] for row in moves]
+            at_y = [[((y ^ m) // 2) * 1024 + ((y ^ m) % 2) * 16 for m in row] for row in moves]
+            at_z = [[(z ^ m) * 32 for m in row] for row in moves]
+            for at, ref in enumerate(fits):
+                part, half = at // 4, (at // 2) % 2
+                if at % 2 != other:
+                    continue
+                cols = slice(CUTS[part], CUTS[part + 1])
+                for j in range(32):
+                    flips = dict(zip(ORDERS[part], (bit(j, 3), bit(j, 4), half)))
+                    rows = at_x[bit(j, 2)][flips["x"]] + at_y[bit(j, 1)][flips["y"]] + at_z[bit(j, 0)][flips["z"]]
+                    place = pl.ds(pl.multiple_of(rows, 16), 16)
+                    high, low = split(ref[j])
+                    fh[place, cols] = high
+                    fl[place, cols] = low
+
+        def narrow(i, carry):
+            rows = pl.ds(pl.multiple_of(i * 32, 32), 32)
+            f8[rows, :] = (fl[rows, :].astype(F32) * F_LOW).astype(F8)
+            f8[pl.ds(pl.multiple_of(q_size + i * 32, 32), 32), :] = (fh[rows, :].astype(F32) * F_HIGH).astype(F8)
+            return carry
+
+        lax.fori_loop(0, q_size // 32, narrow, 0, unroll=2)
         r_ref[...] = jnp.zeros_like(r_ref)
 
-    for i in range(0, a_size, 4):
-        high, low = split(a_ref[i : i + 4].reshape(4 * c_size, a_ref.shape[2]))
-        ah[i * c_size : (i + 4) * c_size, :] = high
-        al[i * c_size : (i + 4) * c_size, :] = low
-    for k in range(k_size):
+    lane = lax.broadcasted_iota(jnp.int32, (a_size, LANES), 1)
+    front, even = lane < 64, (lane // 32) % 2 == 0
+
+    def fit_ready():
+        for i in range(0, a_size, 4):
+            rows = slice(i * c_size, (i + 4) * c_size)
+            value = a_ref[i : i + 4].reshape(4 * c_size, q_size)
+            high = value.astype(BF16)
+            ah[rows, :] = high
+            a8[rows, :q_size] = (value * A_HIGH).astype(F8)
+            a8[rows, q_size:] = ((value - high.astype(F32)) * A_LOW).astype(F8)
+
+    def first_parts():
+        values = [None] * (columns // N_STEP)
+
+        def one(n):
+            cols = slice(n * N_STEP, (n + 1) * N_STEP)
+            values[n] = dot(ah[...], fh[:, cols])
+
+        def rest(n):
+            cols = slice(n * N_STEP, (n + 1) * N_STEP)
+            values[n] = values[n] + dot(a8[...], f8[:, cols]) * UNSCALE
+
+        return values, [functools.partial(f, n) for n in range(len(values)) for f in (one, rest)]
+
+    def store(values):
+        for n, value in enumerate(values):
+            for lt in range(N_STEP // LANES):
+                vs[n * (N_STEP // LANES) + lt] = value[:, lt * LANES : (lt + 1) * LANES]
+
+    def amplitudes_ready(k):
         for at, ref in enumerate(amps):
             half, owner = at // 2, (core if at % 2 == 0 else 1 - core)
             for j in range(4):
@@ -140,64 +175,94 @@
                 th[k, rows, lanes] = high
                 tl[k, rows, lanes] = low
 
-    lane = lax.broadcasted_iota(jnp.int32, (a_size, LANES), 1)
-    front, even = lane < 64, (lane // 32) % 2 == 0
-    for n in range(columns // nt):
-        cols = slice(n * nt, (n + 1) * nt)
-        value = dot3(ah[...], al[...], fh[:, cols], fl[:, cols])
-        for lt in range(lane_tiles):
-            vs[n * lane_tiles + lt] = value[:, lt * LANES : (lt + 1) * LANES]
-        for lt in range(lane_tiles):
-            tile = n * lane_tiles + lt
-            for cq in range(c_size // 4):
-                q = [vs[tile, pl.ds(cq * 4 + j, a_size, stride=c_size), :] for j in range(4)]
-                s = [
-                    jnp.where(front, q[0], pltpu.roll(q[2], 64, 1)),
-                    jnp.where(front, q[1], pltpu.roll(q[3], 64, 1)),
-                    jnp.where(front, pltpu.roll(q[0], 64, 1), q[2]),
-                    jnp.where(front, pltpu.roll(q[1], 64, 1), q[3]),
-                ]
-                w = [
-                    jnp.where(even, s[0], pltpu.roll(s[1], 32, 1)),
-                    jnp.where(even, pltpu.roll(s[0], 96, 1), s[1]),
-                    jnp.where(even, s[2], pltpu.roll(s[3], 32, 1)),
-                    jnp.where(even, pltpu.roll(s[2], 96, 1), s[3]),
-                ]
-                for b in range(4):
-                    high, low = split(w[b])
-                    row = (tile * 4 + b) * a_size
-                    xh[row : row + a_size, cq * LANES : (cq + 1) * LANES] = high
-                    xl[row : row + a_size, cq * LANES : (cq + 1) * LANES] = low
-    for k in range(k_size):
-        rows = slice(k * b_size * a_size, (k + 1) * b_size * a_size)
-        value = dot3(xh[rows, :], xl[rows, :], th[k], tl[k])
-        r_ref[:, k] += value.reshape(b_size, a_size, value.shape[1])
-
-
-def contracted(where, fit_ac, fits, amps, nt=512):
+    def turned(tile, cq):
+        q = [vs[tile, pl.ds(cq * 4 + j, a_size, stride=c_size), :] for j in range(4)]
+        s = [
+            jnp.where(front, q[0], pltpu.roll(q[2], 64, 1)),
+            jnp.where(front, q[1], pltpu.roll(q[3], 64, 1)),
+            jnp.where(front, pltpu.roll(q[0], 64, 1), q[2]),
+            jnp.where(front, pltpu.roll(q[1], 64, 1), q[3]),
+        ]
+        w = [
+            jnp.where(even, s[0], pltpu.roll(s[1], 32, 1)),
+            jnp.where(even, pltpu.roll(s[0], 96, 1), s[1]),
+            jnp.where(even, s[2], pltpu.roll(s[3], 32, 1)),
+            jnp.where(even, pltpu.roll(s[2], 96, 1), s[3]),
+        ]
+        for b in range(4):
+            high, low = split(w[b])
+            row = (tile * 4 + b) * a_size
+            xh[row : row + a_size, cq * LANES : (cq + 1) * LANES] = high
+            xl[row : row + a_size, cq * LANES : (cq + 1) * LANES] = low
+
+    def second_parts():
+        return [functools.partial(amplitudes_ready, k) for k in range(k_size)] + [
+            functools.partial(turned, tile, cq)
+            for tile in range(columns // LANES)
+            for cq in range(c_size // 4)
+        ]
+
+    def second_product():
+        for k in range(k_size):
+            rows = slice(k * b_size * a_size, (k + 1) * b_size * a_size)
+            value = dot3(xh[rows, :], xl[rows, :], th[k], tl[k])
+            r_ref[:, k] += value.reshape(b_size, a_size, pairs)
+
+    @pl.when(step == 0)
+    def _():
+        fit_ready()
+        values, parts = first_parts()
+        for part in parts:
+            part()
+        store(values)
+
+    @pl.when((step > 0) & (step < last))
+    def _():
+        fit_ready()
+        values, dots = first_parts()
+        moves = second_parts()
+        for at, part in enumerate(dots):
+            part()
+            for move in moves[at * len(moves) // len(dots) : (at + 1) * len(moves) // len(dots)]:
+                move()
+        second_product()
+        store(values)
+
+    @pl.when(step == last)
+    def _():
+        for move in second_parts():
+            move()
+        second_product()
+
+
+def contracted(where, fit_ac, fits, amps):
     a_size, c_local, q_size = fit_ac.shape
     k_size, pairs = amps[0].shape[1], amps[0].shape[4]
     columns = CUTS[-1]
     b_size = columns // (k_size * ND)
     rows = a_size * C_STEP
+    steps = c_local // C_STEP
     whole = lambda value: pl.BlockSpec(
         value.shape, lambda i, w: (0,) * value.ndim, pipeline_mode=pl.Buffered(1)
     )
     grid_spec = pltpu.PrefetchScalarGridSpec(
         num_scalar_prefetch=1,
-        grid=(c_local // C_STEP,),
-        in_specs=[pl.BlockSpec((a_size, C_STEP, q_size), lambda i, w: (0, i, 0))]
+        grid=(steps + 1,),
+        in_specs=[pl.BlockSpec((a_size, C_STEP, q_size), lambda i, w: (0, jnp.minimum(i, steps - 1), 0))]
         + [whole(value) for value in fits]
         + [
-            pl.BlockSpec((4, k_size, 2, C_STEP, pairs), lambda i, w: (0, 0, 0, i, 0))
+            pl.BlockSpec(
+                (4, k_size, 2, C_STEP, pairs), lambda i, w: (0, 0, 0, jnp.maximum(i - 1, 0), 0)
+            )
             for _ in amps
         ],
         out_specs=pl.BlockSpec((b_size, k_size, a_size, pairs), lambda i, w: (0, 0, 0, 0)),
         scratch_shapes=[
             pltpu.VMEM((q_size, columns), BF16),
             pltpu.VMEM((q_size, columns), BF16),
+            pltpu.VMEM((2 * q_size, columns), F8),
             pltpu.VMEM((rows, q_size), BF16),
-            pltpu.VMEM((rows, q_size), BF16),
+            pltpu.VMEM((rows, 2 * q_size), F8),
             pltpu.VMEM((k_size * b_size * a_size, C_STEP * ND), BF16),
             pltpu.VMEM((k_size * b_size * a_size, C_STEP * ND), BF16),
             pltpu.VMEM((k_size, C_STEP * ND, pairs), BF16),
@@ -208,7 +273,7 @@
     )
     return pl.pallas_call(
         functools.partial(
-            kernel, n_fit=len(fits), n_amp=len(amps), nt=nt, a_size=a_size, k_size=k_size, b_size=b_size
+            kernel, n_fit=len(fits), n_amp=len(amps), a_size=a_size, k_size=k_size, b_size=b_size
         ),
         grid_spec=grid_spec,
         out_shape=jax.ShapeDtypeStruct((b_size, k_size, a_size, pairs), F32),

time: 142 us -> 128 us (0.901)
  Pallas kernels: 47.9 us -> 34.3 us
    pallas_call x1, Pallas kernels: 47.9 us -> 34.3 us  [contracted(): pl.pallas_call(functools.partial(kernel, n_fit=len(fits), n_amp=len(amps)...]
where the time goes in v2:
time: 128 us
  Pallas kernels  34.3 us (27%)
  starting transfers between devices  33.6 us (26%)
  waiting for transfers between devices  31.1 us (24%)
  blocking collectives  21.5 us (17%)
  other arithmetic  6.23 us (5%)
    pallas_call x1, Pallas kernels, contracted(): pl.pallas_call(functools.partial(kernel, n_fit=len(fits), n_amp=len(amps)...  34.3 us
    ppermute x23, starting transfers between devices, swap(): return lax.ppermute(value, ('aa', 'col'), flipped(move))  33.6 us
    ppermute x23, waiting for transfers between devices, swap(): return lax.ppermute(value, ('aa', 'col'), flipped(move))  31.1 us
    all_to_all x1, blocking collectives, shards(): pieces = lax.all_to_all(pieces, 'col', 0, 0, tiled=True)  21.5 us
    concatenate x11, other arithmetic, grown(): return jnp.concatenate([value, swap(value, move)], axis=0)  4.83 us
  transfers between devices with their start and end apart: 23, of which 11 were waited for; matrix products, arithmetic and copies ran while one was open for 3% of the time, Pallas kernels for 0%

profile of v2, /device:TPU:0, one launch (start us, length us, event | category | flops | bytes accessed | tf_op | source)
XLA Modules:
  0.0 127.9 jit_solution(16235327013923122080)
XLA Ops:
  0.0 2.0 %collective-permute-start = (f32[1,16,1024]{2,1,0:T(8,128)}, f32[1,16,1024]{2,1,0:T(8,128)S(1)}, u32[]{:S(2)}, u32[]{:S(2)}) collective-permute-start(f32[1,16,1024]{2,1,0:T(8,128)} %bitcast.9), channel_id=1, source_target_pairs={{0,2},{8,14},{2,0},{10,12},{4,6},{12,10},{6,4},{14,8},{16,18},{24,... | collective-permute-start | bytes 196616 | tf_op jit(solution)/shard_map/ppermute | solution.py:49
  2.0 2.5 %collective-permute-done = f32[1,16,1024]{2,1,0:T(8,128)S(1)} collective-permute-done((f32[1,16,1024]{2,1,0:T(8,128)}, f32[1,16,1024]{2,1,0:T(8,128)S(1)}, u32[]{:S(2)}, u32[]{:S(2)}) %collective-permute-start) | collective-permute-done | bytes 65568 | tf_op jit(solution)/shard_map/ppermute | solution.py:49
  4.5 0.9 pad_maximum_fusion.11
  5.3 1.7 %collective-permute-start.1 = (f32[2,16,1024]{2,1,0:T(8,128)S(1)}, f32[2,16,1024]{2,1,0:T(8,128)S(1)}, u32[]{:S(2)}, u32[]{:S(2)}) collective-permute-start(f32[2,16,1024]{2,1,0:T(8,128)S(1)} %pad_maximum_fusion.11), channel_id=1, source_target_pairs={{0,1},{8,73},{2,3},{10,75},{4,5},{12,77},{6,7},{14,79},{16,17},{24... | collective-permute-start | bytes 393224 | tf_op jit(solution)/shard_map/ppermute | solution.py:49
  7.1 3.3 %collective-permute-done.1 = f32[2,16,1024]{2,1,0:T(8,128)S(1)} collective-permute-done((f32[2,16,1024]{2,1,0:T(8,128)S(1)}, f32[2,16,1024]{2,1,0:T(8,128)S(1)}, u32[]{:S(2)}, u32[]{:S(2)}) %collective-permute-start.1) | collective-permute-done | bytes 131104 | tf_op jit(solution)/shard_map/ppermute | solution.py:49
  10.4 0.9 pad_maximum_fusion.8
  11.2 1.7 %collective-permute-start.2 = (f32[4,16,1024]{2,1,0:T(8,128)S(1)}, f32[4,16,1024]{2,1,0:T(8,128)S(1)}, u32[]{:S(2)}, u32[]{:S(2)}) collective-permute-start(f32[4,16,1024]{2,1,0:T(8,128)S(1)} %pad_maximum_fusion.8), channel_id=1, source_target_pairs={{0,16},{8,56},{2,18},{10,58},{4,20},{12,60},{6,22},{14,62},{16,0},... | collective-permute-start | bytes 786440 | tf_op jit(solution)/shard_map/ppermute | solution.py:49
  12.9 3.2 %collective-permute-start.18 = (f32[1,2,2,64,256]{4,3,2,1,0:T(8,128)}, f32[1,2,2,64,256]{4,3,2,1,0:T(8,128)S(1)}, u32[]{:S(2)}, u32[]{:S(2)}) collective-permute-start(f32[1,2,2,64,256]{4,3,2,1,0:T(8,128)} %bitcast.14), channel_id=1, source_target_pairs={{0,64},{8,72},{2,66},{10,74},{4,68},{12,76},{6,70},{14,78},{16,80}... | collective-permute-start | bytes 786440 | tf_op jit(solution)/shard_map/ppermute | solution.py:49
  16.1 1.6 %collective-permute-done.2 = f32[4,16,1024]{2,1,0:T(8,128)S(1)} collective-permute-done((f32[4,16,1024]{2,1,0:T(8,128)S(1)}, f32[4,16,1024]{2,1,0:T(8,128)S(1)}, u32[]{:S(2)}, u32[]{:S(2)}) %collective-permute-start.2) | collective-permute-done | bytes 262176 | tf_op jit(solution)/shard_map/ppermute | solution.py:49
  17.7 0.7 pad_maximum_fusion.10
  18.4 4.2 %collective-permute-start.13 = (f32[8,16,256]{2,1,0:T(8,128)S(1)}, f32[8,16,256]{2,1,0:T(8,128)S(1)}, u32[]{:S(2)}, u32[]{:S(2)}) collective-permute-start(f32[8,16,256]{2,1,0:T(8,128)S(1)} %pad_maximum_fusion.10), channel_id=1, source_target_pairs={{0,6},{8,10},{2,4},{10,8},{4,2},{12,14},{6,0},{14,12},{16,22},{24,... | collective-permute-start | bytes 393224 | tf_op jit(solution)/shard_map/ppermute | solution.py:49
  22.6 0.9 pad_maximum_fusion.3
  23.5 3.1 %collective-permute-start.8 = (f32[8,16,384]{2,1,0:T(8,128)S(1)}, f32[8,16,384]{2,1,0:T(8,128)S(1)}, u32[]{:S(2)}, u32[]{:S(2)}) collective-permute-start(f32[8,16,384]{2,1,0:T(8,128)S(1)} %get-tuple-element.5), channel_id=1, source_target_pairs={{0,65},{8,9},{2,67},{10,11},{4,69},{12,13},{6,71},{14,15},{16,81},... | collective-permute-start | bytes 589832 | tf_op jit(solution)/shard_map/ppermute | solution.py:49
  26.6 0.0 collective-permute-done.18
  26.6 1.0 pad_maximum_fusion.5
  27.6 1.6 %collective-permute-start.19 = (f32[2,2,2,64,256]{4,3,2,1,0:T(8,128)S(1)}, f32[2,2,2,64,256]{4,3,2,1,0:T(8,128)S(1)}, u32[]{:S(2)}, u32[]{:S(2)}) collective-permute-start(f32[2,2,2,64,256]{4,3,2,1,0:T(8,128)S(1)} %pad_maximum_fusion.5), channel_id=1, source_target_pairs={{0,16},{8,56},{2,18},{10,58},{4,20},{12,60},{6,22},{14,62},{16,0},... | collective-permute-start | bytes 1572872 | tf_op jit(solution)/shard_map/ppermute | solution.py:49
  29.2 2.1 %collective-permute-start.3 = (f32[8,16,384]{2,1,0:T(8,128)S(1)}, f32[8,16,384]{2,1,0:T(8,128)S(1)}, u32[]{:S(2)}, u32[]{:S(2)}) collective-permute-start(f32[8,16,384]{2,1,0:T(8,128)S(1)} %get-tuple-element.6), channel_id=1, source_target_pairs={{0,48},{8,24},{2,50},{10,26},{4,52},{12,28},{6,54},{14,30},{16,32}... | collective-permute-start | bytes 589832 | tf_op jit(solution)/shard_map/ppermute | solution.py:49
  31.3 0.0 collective-permute-done.13
  31.3 1.2 collective-permute-start.14
  32.5 0.0 collective-permute-done.8
  32.6 0.1 collective-permute-start.9
  32.7 3.5 %collective-permute-done.3 = f32[8,16,384]{2,1,0:T(8,128)S(1)} collective-permute-done((f32[8,16,384]{2,1,0:T(8,128)S(1)}, f32[8,16,384]{2,1,0:T(8,128)S(1)}, u32[]{:S(2)}, u32[]{:S(2)}) %collective-permute-start.3) | collective-permute-done | bytes 196640 | tf_op jit(solution)/shard_map/ppermute | solution.py:49
  36.2 2.3 %collective-permute-start.4 = (f32[16,16,384]{2,1,0:T(8,128)S(1)}, f32[16,16,384]{2,1,0:T(8,128)S(1)}, u32[]{:S(2)}, u32[]{:S(2)}) collective-permute-start(f32[16,16,384]{2,1,0:T(8,128)S(1)} %pad_maximum_fusion.6), channel_id=1, source_target_pairs={{0,65},{8,9},{2,67},{10,11},{4,69},{12,13},{6,71},{14,15},{16,81},... | collective-permute-start | bytes 1179656 | tf_op jit(solution)/shard_map/ppermute | solution.py:49
  38.6 0.4 collective-permute-done.14
  39.1 3.1 %collective-permute-start.16 = (f32[32,16,256]{2,1,0:T(8,128)S(1)}, f32[32,16,256]{2,1,0:T(8,128)}, u32[]{:S(2)}, u32[]{:S(2)}) collective-permute-start(f32[32,16,256]{2,1,0:T(8,128)S(1)} %pad_maximum_fusion.4.refs_10_), channel_id=1, source_target_pairs={{0,65},{8,9},{2,67},{10,11},{4,69},{12,13},{6,71},{14,15},{16,81},... | collective-permute-start | bytes 1572872 | tf_op jit(solution)/shard_map/ppermute | solution.py:49
  42.2 0.0 collective-permute-done.19
  42.2 1.0 pad_maximum_fusion.refs_14_
  43.2 1.5 %collective-permute-start.21 = (f32[4,2,2,64,256]{4,3,2,1,0:T(8,128)S(1)}, f32[4,2,2,64,256]{4,3,2,1,0:T(8,128)}, u32[]{:S(2)}, u32[]{:S(2)}) collective-permute-start(f32[4,2,2,64,256]{4,3,2,1,0:T(8,128)S(1)} %pad_maximum_fusion.refs_14_), channel_id=1, source_target_pairs={{0,48},{8,24},{2,50},{10,26},{4,52},{12,28},{6,54},{14,30},{16,32}... | collective-permute-start | bytes 3145736 | tf_op jit(solution)/shard_map/ppermute | solution.py:49
  44.7 0.0 collective-permute-start.15
  44.7 0.6 collective-permute-done.4
  45.3 0.1 pad_maximum_fusion.1.refs_2_
  45.4 2.6 %collective-permute-start.6 = (f32[32,16,384]{2,1,0:T(8,128)S(1)}, f32[32,16,384]{2,1,0:T(8,128)}, u32[]{:S(2)}, u32[]{:S(2)}) collective-permute-start(f32[32,16,384]{2,1,0:T(8,128)S(1)} %pad_maximum_fusion.1.refs_2_), channel_id=1, source_target_pairs={{0,6},{8,10},{2,4},{10,8},{4,2},{12,14},{6,0},{14,12},{16,22},{24,... | collective-permute-start | bytes 2359304 | tf_op jit(solution)/shard_map/ppermute | solution.py:49
  48.0 0.1 pad_maximum_fusion.2.refs_6_
  48.1 2.9 %collective-permute-done.16.refs_12_ = f32[32,16,256]{2,1,0:T(8,128)} collective-permute-done((f32[32,16,256]{2,1,0:T(8,128)S(1)}, f32[32,16,256]{2,1,0:T(8,128)}, u32[]{:S(2)}, u32[]{:S(2)}) %collective-permute-start.16) | collective-permute-done | bytes 524320 | tf_op jit(solution)/shard_map/ppermute | solution.py:49
  51.0 2.0 %collective-permute-start.11 = (f32[32,16,384]{2,1,0:T(8,128)S(1)}, f32[32,16,384]{2,1,0:T(8,128)}, u32[]{:S(2)}, u32[]{:S(2)}) collective-permute-start(f32[32,16,384]{2,1,0:T(8,128)S(1)} %pad_maximum_fusion.2.refs_6_), channel_id=1, source_target_pairs={{0,48},{8,24},{2,50},{10,26},{4,52},{12,28},{6,54},{14,30},{16,32}... | collective-permute-start | bytes 2359304 | tf_op jit(solution)/shard_map/ppermute | solution.py:49
  53.0 0.0 collective-permute-done.15.refs_11_
  53.0 5.7 %collective-permute-done.6.refs_4_ = f32[32,16,384]{2,1,0:T(8,128)} collective-permute-done((f32[32,16,384]{2,1,0:T(8,128)S(1)}, f32[32,16,384]{2,1,0:T(8,128)}, u32[]{:S(2)}, u32[]{:S(2)}) %collective-permute-start.6) | collective-permute-done | bytes 786464 | tf_op jit(solution)/shard_map/ppermute | solution.py:49
  58.8 0.7 collective-permute-done.21.refs_16_
  59.4 0.5 collective-permute-start.7
  59.9 7.9 %collective-permute-done.11.refs_8_ = f32[32,16,384]{2,1,0:T(8,128)} collective-permute-done((f32[32,16,384]{2,1,0:T(8,128)S(1)}, f32[32,16,384]{2,1,0:T(8,128)}, u32[]{:S(2)}, u32[]{:S(2)}) %collective-permute-start.11) | collective-permute-done | bytes 786464 | tf_op jit(solution)/shard_map/ppermute | solution.py:49
  67.9 0.8 collective-permute-start.17
  68.6 0.1 copy-done.5
  68.7 0.6 pad_add_fusion.refs_0_
  69.3 1.9 %collective-permute-done.17.refs_13_ = f32[32,16,256]{2,1,0:T(8,128)} collective-permute-done((f32[32,16,256]{2,1,0:T(8,128)}, f32[32,16,256]{2,1,0:T(8,128)}, u32[]{:S(2)}, u32[]{:S(2)}) %collective-permute-start.17) | collective-permute-done | bytes 524320 | tf_op jit(solution)/shard_map/ppermute | solution.py:49
  71.3 34.3 %shard_map.37 = f32[16,2,32,256]{3,2,1,0:T(8,128)} custom-call(s32[4]{0:T(128)} %pad_add_fusion.refs_0_, f32[32,64,2048]{2,1,0:T(8,128)} %refs_1_.1, f32[32,16,384]{2,1,0:T(8,128)} %copy-done.1, f32[32,16,384]{2,1,0:T(8,128)} %copy-done.4, f32[32,16,384]{2,1,0:T(8,128)} %collective-permute-done.6.refs_4_, f32[32,16,384]{2,1,0:T(8,128)} %collective-permute-done.7.refs_5_, ...), custom_call_target="tpu_custom_call" | custom-call | tf_op jit(solution)/shard_map/pallas_call | solution.py:274
  105.6 21.5 %all_to_all.5 = f32[8,2,2,32,256]{4,3,2,1,0:T(8,128)S(1)} all-to-all(f32[8,2,2,32,256]{4,3,2,1,0:T(8,128)} %bitcast.8), channel_id=1, replica_groups=mesh['aa'=16,'col'=8] {'col'}, dimensions={0} | all-to-all | bytes 2097152 | tf_op jit(solution)/shard_map/all_to_all | solution.py:314
  127.2 0.1 reduce_sum.9
  127.2 0.7 copy.4
  (30 shorter events, 0.2 us)
Async XLA Ops:
  0.0 4.5 %collective-permute-start = (f32[1,16,1024]{2,1,0:T(8,128)}, f32[1,16,1024]{2,1,0:T(8,128)S(1)}, u32[]{:S(2)}, u32[]{:S(2)}) collective-permute-start(f32[1,16,1024]{2,1,0:T(8,128)} %bitcast.9), channel_id=1, source_target_pairs={{0,2},{8,14},{2,0},{10,12},{4,6},{12,10},{6,4},{14,8},{16,18},{24,... | collective-permute-start | bytes 196616 | tf_op jit(solution)/shard_map/ppermute | solution.py:49
  5.3 5.0 %collective-permute-start.1 = (f32[2,16,1024]{2,1,0:T(8,128)S(1)}, f32[2,16,1024]{2,1,0:T(8,128)S(1)}, u32[]{:S(2)}, u32[]{:S(2)}) collective-permute-start(f32[2,16,1024]{2,1,0:T(8,128)S(1)} %pad_maximum_fusion.11), channel_id=1, source_target_pairs={{0,1},{8,73},{2,3},{10,75},{4,5},{12,77},{6,7},{14,79},{16,17},{24... | collective-permute-start | bytes 393224 | tf_op jit(solution)/shard_map/ppermute | solution.py:49
  11.2 6.5 %collective-permute-start.2 = (f32[4,16,1024]{2,1,0:T(8,128)S(1)}, f32[4,16,1024]{2,1,0:T(8,128)S(1)}, u32[]{:S(2)}, u32[]{:S(2)}) collective-permute-start(f32[4,16,1024]{2,1,0:T(8,128)S(1)} %pad_maximum_fusion.8), channel_id=1, source_target_pairs={{0,16},{8,56},{2,18},{10,58},{4,20},{12,60},{6,22},{14,62},{16,0},... | collective-permute-start | bytes 786440 | tf_op jit(solution)/shard_map/ppermute | solution.py:49
  12.9 13.8 %collective-permute-start.18 = (f32[1,2,2,64,256]{4,3,2,1,0:T(8,128)}, f32[1,2,2,64,256]{4,3,2,1,0:T(8,128)S(1)}, u32[]{:S(2)}, u32[]{:S(2)}) collective-permute-start(f32[1,2,2,64,256]{4,3,2,1,0:T(8,128)} %bitcast.14), channel_id=1, source_target_pairs={{0,64},{8,72},{2,66},{10,74},{4,68},{12,76},{6,70},{14,78},{16,80}... | collective-permute-start | bytes 786440 | tf_op jit(solution)/shard_map/ppermute | solution.py:49
  18.4 12.9 %collective-permute-start.13 = (f32[8,16,256]{2,1,0:T(8,128)S(1)}, f32[8,16,256]{2,1,0:T(8,128)S(1)}, u32[]{:S(2)}, u32[]{:S(2)}) collective-permute-start(f32[8,16,256]{2,1,0:T(8,128)S(1)} %pad_maximum_fusion.10), channel_id=1, source_target_pairs={{0,6},{8,10},{2,4},{10,8},{4,2},{12,14},{6,0},{14,12},{16,22},{24,... | collective-permute-start | bytes 393224 | tf_op jit(solution)/shard_map/ppermute | solution.py:49
  23.5 9.0 %collective-permute-start.8 = (f32[8,16,384]{2,1,0:T(8,128)S(1)}, f32[8,16,384]{2,1,0:T(8,128)S(1)}, u32[]{:S(2)}, u32[]{:S(2)}) collective-permute-start(f32[8,16,384]{2,1,0:T(8,128)S(1)} %get-tuple-element.5), channel_id=1, source_target_pairs={{0,65},{8,9},{2,67},{10,11},{4,69},{12,13},{6,71},{14,15},{16,81},... | collective-permute-start | bytes 589832 | tf_op jit(solution)/shard_map/ppermute | solution.py:49
  27.6 14.5 %collective-permute-start.19 = (f32[2,2,2,64,256]{4,3,2,1,0:T(8,128)S(1)}, f32[2,2,2,64,256]{4,3,2,1,0:T(8,128)S(1)}, u32[]{:S(2)}, u32[]{:S(2)}) collective-permute-start(f32[2,2,2,64,256]{4,3,2,1,0:T(8,128)S(1)} %pad_maximum_fusion.5), channel_id=1, source_target_pairs={{0,16},{8,56},{2,18},{10,58},{4,20},{12,60},{6,22},{14,62},{16,0},... | collective-permute-start | bytes 1572872 | tf_op jit(solution)/shard_map/ppermute | solution.py:49
  29.2 7.0 %collective-permute-start.3 = (f32[8,16,384]{2,1,0:T(8,128)S(1)}, f32[8,16,384]{2,1,0:T(8,128)S(1)}, u32[]{:S(2)}, u32[]{:S(2)}) collective-permute-start(f32[8,16,384]{2,1,0:T(8,128)S(1)} %get-tuple-element.6), channel_id=1, source_target_pairs={{0,48},{8,24},{2,50},{10,26},{4,52},{12,28},{6,54},{14,30},{16,32}... | collective-permute-start | bytes 589832 | tf_op jit(solution)/shard_map/ppermute | solution.py:49
  31.3 7.7 %collective-permute-start.14 = (f32[16,16,256]{2,1,0:T(8,128)S(1)}, f32[16,16,256]{2,1,0:T(8,128)S(1)}, u32[]{:S(2)}, u32[]{:S(2)}) collective-permute-start(f32[16,16,256]{2,1,0:T(8,128)S(1)} %pad_maximum_fusion.9), channel_id=1, source_target_pairs={{0,48},{8,24},{2,50},{10,26},{4,52},{12,28},{6,54},{14,30},{16,32}... | collective-permute-start | bytes 786440 | tf_op jit(solution)/shard_map/ppermute | solution.py:49
  32.6 15.4 %collective-permute-start.9 = (f32[16,16,384]{2,1,0:T(8,128)S(1)}, f32[16,16,384]{2,1,0:T(8,128)S(1)}, u32[]{:S(2)}, u32[]{:S(2)}) collective-permute-start(f32[16,16,384]{2,1,0:T(8,128)S(1)} %pad_maximum_fusion.7), channel_id=1, source_target_pairs={{0,6},{8,10},{2,4},{10,8},{4,2},{12,14},{6,0},{14,12},{16,22},{24,... | collective-permute-start | bytes 1179656 | tf_op jit(solution)/shard_map/ppermute | solution.py:49
  36.2 9.1 %collective-permute-start.4 = (f32[16,16,384]{2,1,0:T(8,128)S(1)}, f32[16,16,384]{2,1,0:T(8,128)S(1)}, u32[]{:S(2)}, u32[]{:S(2)}) collective-permute-start(f32[16,16,384]{2,1,0:T(8,128)S(1)} %pad_maximum_fusion.6), channel_id=1, source_target_pairs={{0,65},{8,9},{2,67},{10,11},{4,69},{12,13},{6,71},{14,15},{16,81},... | collective-permute-start | bytes 1179656 | tf_op jit(solution)/shard_map/ppermute | solution.py:49
  39.1 32.2 %copy-start.3 = (f32[32,16,256]{2,1,0:T(8,128)}, f32[32,16,256]{2,1,0:T(8,128)S(1)}, u32[]{:S(2)}) copy-start(f32[32,16,256]{2,1,0:T(8,128)S(1)} %pad_maximum_fusion.4.refs_10_) | copy-start | bytes 1572868
  39.1 12.0 %collective-permute-start.16 = (f32[32,16,256]{2,1,0:T(8,128)S(1)}, f32[32,16,256]{2,1,0:T(8,128)}, u32[]{:S(2)}, u32[]{:S(2)}) collective-permute-start(f32[32,16,256]{2,1,0:T(8,128)S(1)} %pad_maximum_fusion.4.refs_10_), channel_id=1, source_target_pairs={{0,65},{8,9},{2,67},{10,11},{4,69},{12,13},{6,71},{14,15},{16,81},... | collective-permute-start | bytes 1572872 | tf_op jit(solution)/shard_map/ppermute | solution.py:49
  43.2 28.0 %copy-start = (f32[4,2,2,64,256]{4,3,2,1,0:T(8,128)}, f32[4,2,2,64,256]{4,3,2,1,0:T(8,128)S(1)}, u32[]{:S(2)}) copy-start(f32[4,2,2,64,256]{4,3,2,1,0:T(8,128)S(1)} %pad_maximum_fusion.refs_14_) | copy-start | bytes 3145732
  43.2 16.2 %collective-permute-start.21 = (f32[4,2,2,64,256]{4,3,2,1,0:T(8,128)S(1)}, f32[4,2,2,64,256]{4,3,2,1,0:T(8,128)}, u32[]{:S(2)}, u32[]{:S(2)}) collective-permute-start(f32[4,2,2,64,256]{4,3,2,1,0:T(8,128)S(1)} %pad_maximum_fusion.refs_14_), channel_id=1, source_target_pairs={{0,48},{8,24},{2,50},{10,26},{4,52},{12,28},{6,54},{14,30},{16,32}... | collective-permute-start | bytes 3145736 | tf_op jit(solution)/shard_map/ppermute | solution.py:49
  44.7 8.3 %collective-permute-start.15 = (f32[32,16,256]{2,1,0:T(8,128)S(1)}, f32[32,16,256]{2,1,0:T(8,128)S(1)}, u32[]{:S(2)}, u32[]{:S(2)}) collective-permute-start(f32[32,16,256]{2,1,0:T(8,128)S(1)} %pad_maximum_fusion.4.refs_10_), channel_id=1, source_target_pairs={{0,8},{8,0},{2,10},{10,2},{4,12},{12,4},{6,14},{14,6},{16,24},{24,... | collective-permute-start | bytes 1572872 | tf_op jit(solution)/shard_map/ppermute | solution.py:49
  45.4 25.9 %copy-start.1 = (f32[32,16,384]{2,1,0:T(8,128)}, f32[32,16,384]{2,1,0:T(8,128)S(1)}, u32[]{:S(2)}) copy-start(f32[32,16,384]{2,1,0:T(8,128)S(1)} %pad_maximum_fusion.1.refs_2_) | copy-start | bytes 2359300
  45.4 13.4 %collective-permute-start.6 = (f32[32,16,384]{2,1,0:T(8,128)S(1)}, f32[32,16,384]{2,1,0:T(8,128)}, u32[]{:S(2)}, u32[]{:S(2)}) collective-permute-start(f32[32,16,384]{2,1,0:T(8,128)S(1)} %pad_maximum_fusion.1.refs_2_), channel_id=1, source_target_pairs={{0,6},{8,10},{2,4},{10,8},{4,2},{12,14},{6,0},{14,12},{16,22},{24,... | collective-permute-start | bytes 2359304 | tf_op jit(solution)/shard_map/ppermute | solution.py:49
  48.0 11.4 %collective-permute-start.5 = (f32[32,16,384]{2,1,0:T(8,128)S(1)}, f32[32,16,384]{2,1,0:T(8,128)S(1)}, u32[]{:S(2)}, u32[]{:S(2)}) collective-permute-start(f32[32,16,384]{2,1,0:T(8,128)S(1)} %pad_maximum_fusion.1.refs_2_), channel_id=1, source_target_pairs={{0,8},{8,0},{2,10},{10,2},{4,12},{12,4},{6,14},{14,6},{16,24},{24,... | collective-permute-start | bytes 2359304 | tf_op jit(solution)/shard_map/ppermute | solution.py:49
  48.1 23.2 %copy-start.2 = (f32[32,16,384]{2,1,0:T(8,128)}, f32[32,16,384]{2,1,0:T(8,128)S(1)}, u32[]{:S(2)}) copy-start(f32[32,16,384]{2,1,0:T(8,128)S(1)} %pad_maximum_fusion.2.refs_6_) | copy-start | bytes 2359300
  51.0 16.8 %collective-permute-start.11 = (f32[32,16,384]{2,1,0:T(8,128)S(1)}, f32[32,16,384]{2,1,0:T(8,128)}, u32[]{:S(2)}, u32[]{:S(2)}) collective-permute-start(f32[32,16,384]{2,1,0:T(8,128)S(1)} %pad_maximum_fusion.2.refs_6_), channel_id=1, source_target_pairs={{0,48},{8,24},{2,50},{10,26},{4,52},{12,28},{6,54},{14,30},{16,32}... | collective-permute-start | bytes 2359304 | tf_op jit(solution)/shard_map/ppermute | solution.py:49
  53.0 15.6 %copy-start.6 = (f32[32,16,256]{2,1,0:T(8,128)}, f32[32,16,256]{2,1,0:T(8,128)S(1)}, u32[]{:S(2)}) copy-start(f32[32,16,256]{2,1,0:T(8,128)S(1)} %collective-permute-done.15.refs_11_) | copy-start | bytes 1572868
  53.0 14.8 %collective-permute-start.10 = (f32[32,16,384]{2,1,0:T(8,128)S(1)}, f32[32,16,384]{2,1,0:T(8,128)S(1)}, u32[]{:S(2)}, u32[]{:S(2)}) collective-permute-start(f32[32,16,384]{2,1,0:T(8,128)S(1)} %pad_maximum_fusion.2.refs_6_), channel_id=1, source_target_pairs={{0,8},{8,0},{2,10},{10,2},{4,12},{12,4},{6,14},{14,6},{16,24},{24,... | collective-permute-start | bytes 2359304 | tf_op jit(solution)/shard_map/ppermute | solution.py:49
  58.8 10.6 %collective-permute-start.20 = (f32[4,2,2,64,256]{4,3,2,1,0:T(8,128)S(1)}, f32[4,2,2,64,256]{4,3,2,1,0:T(8,128)}, u32[]{:S(2)}, u32[]{:S(2)}) collective-permute-start(f32[4,2,2,64,256]{4,3,2,1,0:T(8,128)S(1)} %pad_maximum_fusion.refs_14_), channel_id=1, source_target_pairs={{0,8},{8,0},{2,10},{10,2},{4,12},{12,4},{6,14},{14,6},{16,24},{24,... | collective-permute-start | bytes 3145736 | tf_op jit(solution)/shard_map/ppermute | solution.py:49
  59.4 11.8 %collective-permute-start.22 = (f32[4,2,2,64,256]{4,3,2,1,0:T(8,128)}, f32[4,2,2,64,256]{4,3,2,1,0:T(8,128)}, u32[]{:S(2)}, u32[]{:S(2)}) collective-permute-start(f32[4,2,2,64,256]{4,3,2,1,0:T(8,128)} %collective-permute-done.21.refs_16_), channel_id=1, source_target_pairs={{0,8},{8,0},{2,10},{10,2},{4,12},{12,4},{6,14},{14,6},{16,24},{24,... | collective-permute-start | bytes 3145736 | tf_op jit(solution)/shard_map/ppermute | solution.py:49
  59.4 8.4 %copy-start.4 = (f32[32,16,384]{2,1,0:T(8,128)}, f32[32,16,384]{2,1,0:T(8,128)S(1)}, u32[]{:S(2)}) copy-start(f32[32,16,384]{2,1,0:T(8,128)S(1)} %collective-permute-done.5.refs_3_) | copy-start | bytes 2359300
  59.4 11.8 %collective-permute-start.7 = (f32[32,16,384]{2,1,0:T(8,128)}, f32[32,16,384]{2,1,0:T(8,128)}, u32[]{:S(2)}, u32[]{:S(2)}) collective-permute-start(f32[32,16,384]{2,1,0:T(8,128)} %collective-permute-done.6.refs_4_), channel_id=1, source_target_pairs={{0,8},{8,0},{2,10},{10,2},{4,12},{12,4},{6,14},{14,6},{16,24},{24,... | collective-permute-start | bytes 2359304 | tf_op jit(solution)/shard_map/ppermute | solution.py:49
  67.8 3.4 %collective-permute-start.12 = (f32[32,16,384]{2,1,0:T(8,128)}, f32[32,16,384]{2,1,0:T(8,128)}, u32[]{:S(2)}, u32[]{:S(2)}) collective-permute-start(f32[32,16,384]{2,1,0:T(8,128)} %collective-permute-done.11.refs_8_), channel_id=1, source_target_pairs={{0,8},{8,0},{2,10},{10,2},{4,12},{12,4},{6,14},{14,6},{16,24},{24,... | collective-permute-start | bytes 2359304 | tf_op jit(solution)/shard_map/ppermute | solution.py:49
  67.9 0.9 copy-start.5
  67.9 3.4 %collective-permute-start.17 = (f32[32,16,256]{2,1,0:T(8,128)}, f32[32,16,256]{2,1,0:T(8,128)}, u32[]{:S(2)}, u32[]{:S(2)}) collective-permute-start(f32[32,16,256]{2,1,0:T(8,128)} %collective-permute-done.16.refs_12_), channel_id=1, source_target_pairs={{0,8},{8,0},{2,10},{10,2},{4,12},{12,4},{6,14},{14,6},{16,24},{24,... | collective-permute-start | bytes 1572872 | tf_op jit(solution)/shard_map/ppermute | solution.py:49

commit v3 on v2

--- a/solution.py
+++ b/solution.py
@@ -103,10 +103,15 @@
         for other in range(2):
             owner = core if other == 0 else 1 - core
             first, second = chosen(owner, FIRST), chosen(owner, SECOND)
-            moves = [[0, second], [first, first ^ second]]
-            at_x = [[(x ^ m) * 256 + owner * 128 for m in row] for row in moves]
-            at_y = [[((y ^ m) // 2) * 1024 + ((y ^ m) % 2) * 16 for m in row] for row in moves]
-            at_z = [[(z ^ m) * 32 for m in row] for row in moves]
+
+            def reached(at):
+                froms = [at, at ^ second]
+                lower = [jnp.minimum(v, v ^ first) for v in froms]
+                return [lower, [v ^ first for v in lower]]
+
+            at_x = [[v * 256 + owner * 128 for v in row] for row in reached(x)]
+            at_y = [[(v // 2) * 1024 + (v % 2) * 16 for v in row] for row in reached(y)]
+            at_z = [[v * 32 for v in row] for row in reached(z)]
             for at, ref in enumerate(fits):
                 part, half = at // 4, (at // 2) % 2
                 if at % 2 != other:
@@ -281,10 +286,24 @@
     )(where, fit_ac, *fits, *amps)
 
 
+def sent_to_all(value, groups):
+    copies = jnp.broadcast_to(value, (len(groups[0]), *value.shape))
+    return lax.all_to_all(copies, ("aa", "col"), 0, 0, tiled=True, axis_index_groups=groups)
+
+
+def cubes():
+    pairs = [[(0, 1), (2, 3)], [(0, 3), (1, 2)]]
+    return [
+        [device_at(x, y, z, core) for x in xs for y in ys for z in zs]
+        for core in range(2)
+        for xs in pairs[core]
+        for ys in pairs[core]
+        for zs in pairs[core]
+    ]
+
+
 def gathered_fit(fit_bd):
-    value = fit_bd[None]
-    for move in ("z1", "y1", "x1"):
-        value = grown(value, move)
+    value = sent_to_all(fit_bd, cubes())
     parts = [value[:, :, CUTS[i] : CUTS[i + 1]] for i in range(3)]
     for at in range(2):
         parts = [grown(part, order[at] + "2") for part, order in zip(parts, ORDERS)]

time: 128 us -> 124 us (0.969)
  waiting for transfers between devices: 31.1 us -> 24.4 us
  other arithmetic: 6.23 us -> 3.03 us
  starting transfers between devices: 33.6 us -> 35.9 us
  local copies, waits for them, and re-layouts: 0.84 us -> 3.03 us
  blocking collectives: 21.5 us -> 23.2 us
    ppermute x23 -> x20, waiting for transfers between devices: 31.1 us -> 19.5 us  [swap(): return lax.ppermute(value, ('aa', 'col'), flipped(move))]
    all_to_all x0 -> x1, starting transfers between devices: none -> 5.22 us  [sent_to_all(): lax.all_to_all(copies, ('aa', 'col'), 0, 0, tiled=True, axis_index_groups...]
    all_to_all x0 -> x1, waiting for transfers between devices: none -> 4.85 us  [sent_to_all(): lax.all_to_all(copies, ('aa', 'col'), 0, 0, tiled=True, axis_index_groups...]
    ppermute x23 -> x20, starting transfers between devices: 33.6 us -> 30.7 us  [swap(): return lax.ppermute(value, ('aa', 'col'), flipped(move))]
    concatenate x11 -> x8, other arithmetic: 4.83 us -> 2.32 us  [grown(): return jnp.concatenate([value, swap(value, move)], axis=0)]
    broadcast_in_dim x0 -> x1, local copies, waits for them, and re-layouts: none -> 1.7 us  [sent_to_all(): copies = jnp.broadcast_to(value, (len(groups[0]), *value.shape))]
    all_to_all x1, blocking collectives: 21.5 us -> 23.2 us  [shards(): pieces = lax.all_to_all(pieces, 'col', 0, 0, tiled=True)]
  transfers between devices with their start and end apart: 23 -> 21, of which waited for: 11 -> 7; matrix products, arithmetic and copies ran while one was open for 3% -> 2% of each run, Pallas kernels for 0% -> 0%
where the time goes in v3:
time: 124 us
  starting transfers between devices  35.9 us (29%)
  Pallas kernels  34.3 us (28%)
  waiting for transfers between devices  24.4 us (20%)
  blocking collectives  23.2 us (19%)
  local copies, waits for them, and re-layouts  3.03 us (2%)
  other arithmetic  3.03 us (2%)
    pallas_call x1, Pallas kernels, contracted(): pl.pallas_call(functools.partial(kernel, n_fit=len(fits), n_amp=len(amps)...  34.3 us
    ppermute x20, starting transfers between devices, swap(): return lax.ppermute(value, ('aa', 'col'), flipped(move))  30.7 us
    all_to_all x1, blocking collectives, shards(): pieces = lax.all_to_all(pieces, 'col', 0, 0, tiled=True)  23.2 us
    ppermute x20, waiting for transfers between devices, swap(): return lax.ppermute(value, ('aa', 'col'), flipped(move))  19.5 us
    all_to_all x1, starting transfers between devices, sent_to_all(): lax.all_to_all(copies, ('aa', 'col'), 0, 0, tiled=True, axis_index_groups...  5.22 us
    all_to_all x1, waiting for transfers between devices, sent_to_all(): lax.all_to_all(copies, ('aa', 'col'), 0, 0, tiled=True, axis_index_groups...  4.85 us
  transfers between devices with their start and end apart: 21, of which 7 were waited for; matrix products, arithmetic and copies ran while one was open for 2% of the time, Pallas kernels for 0%

profile of v3, /device:TPU:0, one launch (start us, length us, event | category | flops | bytes accessed | tf_op | source)
XLA Modules:
  0.0 124.0 jit_solution(9288289154678848231)
XLA Ops:
  0.0 1.7 %broadcast_in_dim.6 = f32[8,16,1024]{2,1,0:T(8,128)} broadcast(f32[16,1024]{1,0:T(8,128)} %param.4), dimensions={1,2} | broadcast | bytes 589824 | tf_op jit(solution)/shard_map/broadcast_in_dim | solution.py:290
  1.7 5.2 %all-to-all-start = ((f32[8,16,1024]{2,1,0:T(8,128)}), f32[8,16,1024]{2,1,0:T(8,128)S(1)}, u32[]{:S(2)}, u32[]{:S(2)}) async-start(f32[8,16,1024]{2,1,0:T(8,128)} %broadcast_in_dim.6), calls=%async_computation | async-start | bytes 1048576 | tf_op jit(solution)/shard_map/all_to_all | solution.py:291
  6.9 2.9 %collective-permute-start.15 = (f32[1,2,2,64,256]{4,3,2,1,0:T(8,128)}, f32[1,2,2,64,256]{4,3,2,1,0:T(8,128)S(1)}, u32[]{:S(2)}, u32[]{:S(2)}) collective-permute-start(f32[1,2,2,64,256]{4,3,2,1,0:T(8,128)} %bitcast.8), channel_id=1, source_target_pairs={{0,64},{8,72},{2,66},{10,74},{4,68},{12,76},{6,70},{14,78},{16,80}... | collective-permute-start | bytes 786440 | tf_op jit(solution)/shard_map/ppermute | solution.py:49
  9.8 4.8 %all-to-all-done = f32[8,16,1024]{2,1,0:T(8,128)S(1)} async-done(((f32[8,16,1024]{2,1,0:T(8,128)}), f32[8,16,1024]{2,1,0:T(8,128)S(1)}, u32[]{:S(2)}, u32[]{:S(2)}) %all-to-all-start) | async-done | bytes 524320 | tf_op jit(solution)/shard_map/all_to_all | solution.py:291
  14.7 2.5 %collective-permute-start.10 = (f32[8,16,256]{2,1,0:T(8,128)S(1)}, f32[8,16,256]{2,1,0:T(8,128)S(1)}, u32[]{:S(2)}, u32[]{:S(2)}) collective-permute-start(f32[8,16,256]{2,1,0:T(8,128)S(1)} %slice.14), channel_id=1, source_target_pairs={{0,6},{8,10},{2,4},{10,8},{4,2},{12,14},{6,0},{14,12},{16,22},{24,... | collective-permute-start | bytes 393224 | tf_op jit(solution)/shard_map/ppermute | solution.py:49
  17.2 3.0 %collective-permute-start.5 = (f32[8,16,384]{2,1,0:T(8,128)S(1)}, f32[8,16,384]{2,1,0:T(8,128)S(1)}, u32[]{:S(2)}, u32[]{:S(2)}) collective-permute-start(f32[8,16,384]{2,1,0:T(8,128)S(1)} %get-tuple-element.5), channel_id=1, source_target_pairs={{0,65},{8,9},{2,67},{10,11},{4,69},{12,13},{6,71},{14,15},{16,81},... | collective-permute-start | bytes 589832 | tf_op jit(solution)/shard_map/ppermute | solution.py:49
  20.2 0.0 collective-permute-done.15
  20.2 1.0 pad_maximum_fusion.4
  21.2 2.7 %collective-permute-start.16 = (f32[2,2,2,64,256]{4,3,2,1,0:T(8,128)S(1)}, f32[2,2,2,64,256]{4,3,2,1,0:T(8,128)S(1)}, u32[]{:S(2)}, u32[]{:S(2)}) collective-permute-start(f32[2,2,2,64,256]{4,3,2,1,0:T(8,128)S(1)} %pad_maximum_fusion.4), channel_id=1, source_target_pairs={{0,16},{8,56},{2,18},{10,58},{4,20},{12,60},{6,22},{14,62},{16,0},... | collective-permute-start | bytes 1572872 | tf_op jit(solution)/shard_map/ppermute | solution.py:49
  24.0 1.1 collective-permute-start
  25.1 0.0 collective-permute-done.10
  25.1 2.2 %collective-permute-start.11 = (f32[16,16,256]{2,1,0:T(8,128)S(1)}, f32[16,16,256]{2,1,0:T(8,128)S(1)}, u32[]{:S(2)}, u32[]{:S(2)}) collective-permute-start(f32[16,16,256]{2,1,0:T(8,128)S(1)} %pad_maximum_fusion.7), channel_id=1, source_target_pairs={{0,48},{8,24},{2,50},{10,26},{4,52},{12,28},{6,54},{14,30},{16,32}... | collective-permute-start | bytes 786440 | tf_op jit(solution)/shard_map/ppermute | solution.py:49
  27.3 4.4 %collective-permute-start.6 = (f32[16,16,384]{2,1,0:T(8,128)S(1)}, f32[16,16,384]{2,1,0:T(8,128)S(1)}, u32[]{:S(2)}, u32[]{:S(2)}) collective-permute-start(f32[16,16,384]{2,1,0:T(8,128)S(1)} %pad_maximum_fusion.6), channel_id=1, source_target_pairs={{0,6},{8,10},{2,4},{10,8},{4,2},{12,14},{6,0},{14,12},{16,22},{24,... | collective-permute-start | bytes 1179656 | tf_op jit(solution)/shard_map/ppermute | solution.py:49
  31.7 0.0 collective-permute-done
  31.8 0.1 collective-permute-start.1
  31.8 4.2 %collective-permute-done.11 = f32[16,16,256]{2,1,0:T(8,128)S(1)} collective-permute-done((f32[16,16,256]{2,1,0:T(8,128)S(1)}, f32[16,16,256]{2,1,0:T(8,128)S(1)}, u32[]{:S(2)}, u32[]{:S(2)}) %collective-permute-start.11) | collective-permute-done | bytes 262176 | tf_op jit(solution)/shard_map/ppermute | solution.py:49
  36.1 0.1 collective-permute-start.13
  36.2 1.1 pad_maximum_fusion.refs_14_
  37.4 0.2 collective-permute-start.18
  37.6 3.1 %collective-permute-start.12 = (f32[32,16,256]{2,1,0:T(8,128)S(1)}, f32[32,16,256]{2,1,0:T(8,128)S(1)}, u32[]{:S(2)}, u32[]{:S(2)}) collective-permute-start(f32[32,16,256]{2,1,0:T(8,128)S(1)} %pad_maximum_fusion.3.refs_10_), channel_id=1, source_target_pairs={{0,8},{8,0},{2,10},{10,2},{4,12},{12,4},{6,14},{14,6},{16,24},{24,... | collective-permute-start | bytes 1572872 | tf_op jit(solution)/shard_map/ppermute | solution.py:49
  40.6 0.2 collective-permute-done.1
  40.8 0.1 pad_maximum_fusion.1.refs_2_
  40.9 5.7 %collective-permute-start.3 = (f32[32,16,384]{2,1,0:T(8,128)S(1)}, f32[32,16,384]{2,1,0:T(8,128)}, u32[]{:S(2)}, u32[]{:S(2)}) collective-permute-start(f32[32,16,384]{2,1,0:T(8,128)S(1)} %pad_maximum_fusion.1.refs_2_), channel_id=1, source_target_pairs={{0,6},{8,10},{2,4},{10,8},{4,2},{12,14},{6,0},{14,12},{16,22},{24,... | collective-permute-start | bytes 2359304 | tf_op jit(solution)/shard_map/ppermute | solution.py:49
  46.6 0.0 collective-permute-done.6
  46.6 0.0 collective-permute-start.2
  46.6 0.1 pad_maximum_fusion.2.refs_6_
  46.6 0.1 collective-permute-done.13.refs_12_
  46.7 1.1 collective-permute-start.8
  47.8 0.0 collective-permute-start.7
  47.8 8.8 %collective-permute-done.3.refs_4_ = f32[32,16,384]{2,1,0:T(8,128)} collective-permute-done((f32[32,16,384]{2,1,0:T(8,128)S(1)}, f32[32,16,384]{2,1,0:T(8,128)}, u32[]{:S(2)}, u32[]{:S(2)}) %collective-permute-start.3) | collective-permute-done | bytes 786464 | tf_op jit(solution)/shard_map/ppermute | solution.py:49
  56.6 0.0 collective-permute-start.17
  56.6 0.0 collective-permute-done.18.refs_16_
  56.6 0.5 collective-permute-start.19
  57.1 0.0 collective-permute-done.2.refs_3_
  57.2 0.1 collective-permute-start.4
  57.2 4.7 %collective-permute-done.8.refs_8_ = f32[32,16,384]{2,1,0:T(8,128)} collective-permute-done((f32[32,16,384]{2,1,0:T(8,128)S(1)}, f32[32,16,384]{2,1,0:T(8,128)}, u32[]{:S(2)}, u32[]{:S(2)}) %collective-permute-start.8) | collective-permute-done | bytes 786464 | tf_op jit(solution)/shard_map/ppermute | solution.py:49
  62.0 0.7 collective-permute-start.9
  62.7 0.0 collective-permute-done.7.refs_7_
  62.7 0.3 collective-permute-start.14
  63.0 0.6 copy-done.5
  63.6 0.6 pad_add_fusion.refs_0_
  64.2 1.5 %collective-permute-done.14.refs_13_ = f32[32,16,256]{2,1,0:T(8,128)} collective-permute-done((f32[32,16,256]{2,1,0:T(8,128)}, f32[32,16,256]{2,1,0:T(8,128)}, u32[]{:S(2)}, u32[]{:S(2)}) %collective-permute-start.14) | collective-permute-done | bytes 524320 | tf_op jit(solution)/shard_map/ppermute | solution.py:49
  65.7 0.0 collective-permute-done.4.refs_5_
  65.7 0.0 collective-permute-done.9.refs_9_
  65.8 34.3 %shard_map.37 = f32[16,2,32,256]{3,2,1,0:T(8,128)} custom-call(s32[4]{0:T(128)} %pad_add_fusion.refs_0_, f32[32,64,2048]{2,1,0:T(8,128)} %refs_1_.1, f32[32,16,384]{2,1,0:T(8,128)} %copy-done.1, f32[32,16,384]{2,1,0:T(8,128)} %copy-done.4, f32[32,16,384]{2,1,0:T(8,128)} %collective-permute-done.3.refs_4_, f32[32,16,384]{2,1,0:T(8,128)} %collective-permute-done.4.refs_5_, ...), custom_call_target="tpu_custom_call" | custom-call | tf_op jit(solution)/shard_map/pallas_call | solution.py:279
  100.1 23.2 %all_to_all.10 = f32[8,2,2,32,256]{4,3,2,1,0:T(8,128)S(1)} all-to-all(f32[8,2,2,32,256]{4,3,2,1,0:T(8,128)} %bitcast.7), channel_id=1, replica_groups=mesh['aa'=16,'col'=8] {'col'}, dimensions={0} | all-to-all | bytes 2097152 | tf_op jit(solution)/shard_map/all_to_all | solution.py:333
  123.3 0.1 reduce_sum.9
  123.4 0.7 copy.4
  (24 shorter events, 0.2 us)
Async XLA Ops:
  1.7 13.0 %all-to-all-start = ((f32[8,16,1024]{2,1,0:T(8,128)}), f32[8,16,1024]{2,1,0:T(8,128)S(1)}, u32[]{:S(2)}, u32[]{:S(2)}) async-start(f32[8,16,1024]{2,1,0:T(8,128)} %broadcast_in_dim.6), calls=%async_computation | async-start | bytes 1048576 | tf_op jit(solution)/shard_map/all_to_all | solution.py:291
  6.9 13.3 %collective-permute-start.15 = (f32[1,2,2,64,256]{4,3,2,1,0:T(8,128)}, f32[1,2,2,64,256]{4,3,2,1,0:T(8,128)S(1)}, u32[]{:S(2)}, u32[]{:S(2)}) collective-permute-start(f32[1,2,2,64,256]{4,3,2,1,0:T(8,128)} %bitcast.8), channel_id=1, source_target_pairs={{0,64},{8,72},{2,66},{10,74},{4,68},{12,76},{6,70},{14,78},{16,80}... | collective-permute-start | bytes 786440 | tf_op jit(solution)/shard_map/ppermute | solution.py:49
  14.7 10.4 %collective-permute-start.10 = (f32[8,16,256]{2,1,0:T(8,128)S(1)}, f32[8,16,256]{2,1,0:T(8,128)S(1)}, u32[]{:S(2)}, u32[]{:S(2)}) collective-permute-start(f32[8,16,256]{2,1,0:T(8,128)S(1)} %slice.14), channel_id=1, source_target_pairs={{0,6},{8,10},{2,4},{10,8},{4,2},{12,14},{6,0},{14,12},{16,22},{24,... | collective-permute-start | bytes 393224 | tf_op jit(solution)/shard_map/ppermute | solution.py:49
  17.2 10.1 %collective-permute-start.5 = (f32[8,16,384]{2,1,0:T(8,128)S(1)}, f32[8,16,384]{2,1,0:T(8,128)S(1)}, u32[]{:S(2)}, u32[]{:S(2)}) collective-permute-start(f32[8,16,384]{2,1,0:T(8,128)S(1)} %get-tuple-element.5), channel_id=1, source_target_pairs={{0,65},{8,9},{2,67},{10,11},{4,69},{12,13},{6,71},{14,15},{16,81},... | collective-permute-start | bytes 589832 | tf_op jit(solution)/shard_map/ppermute | solution.py:49
  21.2 15.0 %collective-permute-start.16 = (f32[2,2,2,64,256]{4,3,2,1,0:T(8,128)S(1)}, f32[2,2,2,64,256]{4,3,2,1,0:T(8,128)S(1)}, u32[]{:S(2)}, u32[]{:S(2)}) collective-permute-start(f32[2,2,2,64,256]{4,3,2,1,0:T(8,128)S(1)} %pad_maximum_fusion.4), channel_id=1, source_target_pairs={{0,16},{8,56},{2,18},{10,58},{4,20},{12,60},{6,22},{14,62},{16,0},... | collective-permute-start | bytes 1572872 | tf_op jit(solution)/shard_map/ppermute | solution.py:49
  24.0 7.8 %collective-permute-start = (f32[8,16,384]{2,1,0:T(8,128)S(1)}, f32[8,16,384]{2,1,0:T(8,128)S(1)}, u32[]{:S(2)}, u32[]{:S(2)}) collective-permute-start(f32[8,16,384]{2,1,0:T(8,128)S(1)} %get-tuple-element.6), channel_id=1, source_target_pairs={{0,48},{8,24},{2,50},{10,26},{4,52},{12,28},{6,54},{14,30},{16,32}... | collective-permute-start | bytes 589832 | tf_op jit(solution)/shard_map/ppermute | solution.py:49
  25.1 11.0 %collective-permute-start.11 = (f32[16,16,256]{2,1,0:T(8,128)S(1)}, f32[16,16,256]{2,1,0:T(8,128)S(1)}, u32[]{:S(2)}, u32[]{:S(2)}) collective-permute-start(f32[16,16,256]{2,1,0:T(8,128)S(1)} %pad_maximum_fusion.7), channel_id=1, source_target_pairs={{0,48},{8,24},{2,50},{10,26},{4,52},{12,28},{6,54},{14,30},{16,32}... | collective-permute-start | bytes 786440 | tf_op jit(solution)/shard_map/ppermute | solution.py:49
  27.3 19.2 %collective-permute-start.6 = (f32[16,16,384]{2,1,0:T(8,128)S(1)}, f32[16,16,384]{2,1,0:T(8,128)S(1)}, u32[]{:S(2)}, u32[]{:S(2)}) collective-permute-start(f32[16,16,384]{2,1,0:T(8,128)S(1)} %pad_maximum_fusion.6), channel_id=1, source_target_pairs={{0,6},{8,10},{2,4},{10,8},{4,2},{12,14},{6,0},{14,12},{16,22},{24,... | collective-permute-start | bytes 1179656 | tf_op jit(solution)/shard_map/ppermute | solution.py:49
  31.8 9.1 %collective-permute-start.1 = (f32[16,16,384]{2,1,0:T(8,128)S(1)}, f32[16,16,384]{2,1,0:T(8,128)S(1)}, u32[]{:S(2)}, u32[]{:S(2)}) collective-permute-start(f32[16,16,384]{2,1,0:T(8,128)S(1)} %pad_maximum_fusion.5), channel_id=1, source_target_pairs={{0,65},{8,9},{2,67},{10,11},{4,69},{12,13},{6,71},{14,15},{16,81},... | collective-permute-start | bytes 1179656 | tf_op jit(solution)/shard_map/ppermute | solution.py:49
  36.1 29.6 %copy-start.3 = (f32[32,16,256]{2,1,0:T(8,128)}, f32[32,16,256]{2,1,0:T(8,128)S(1)}, u32[]{:S(2)}) copy-start(f32[32,16,256]{2,1,0:T(8,128)S(1)} %pad_maximum_fusion.3.refs_10_) | copy-start | bytes 1572868
  36.1 10.6 %collective-permute-start.13 = (f32[32,16,256]{2,1,0:T(8,128)S(1)}, f32[32,16,256]{2,1,0:T(8,128)}, u32[]{:S(2)}, u32[]{:S(2)}) collective-permute-start(f32[32,16,256]{2,1,0:T(8,128)S(1)} %pad_maximum_fusion.3.refs_10_), channel_id=1, source_target_pairs={{0,65},{8,9},{2,67},{10,11},{4,69},{12,13},{6,71},{14,15},{16,81},... | collective-permute-start | bytes 1572872 | tf_op jit(solution)/shard_map/ppermute | solution.py:49
  37.4 28.4 %copy-start = (f32[4,2,2,64,256]{4,3,2,1,0:T(8,128)}, f32[4,2,2,64,256]{4,3,2,1,0:T(8,128)S(1)}, u32[]{:S(2)}) copy-start(f32[4,2,2,64,256]{4,3,2,1,0:T(8,128)S(1)} %pad_maximum_fusion.refs_14_) | copy-start | bytes 3145732
  37.4 19.3 %collective-permute-start.18 = (f32[4,2,2,64,256]{4,3,2,1,0:T(8,128)S(1)}, f32[4,2,2,64,256]{4,3,2,1,0:T(8,128)}, u32[]{:S(2)}, u32[]{:S(2)}) collective-permute-start(f32[4,2,2,64,256]{4,3,2,1,0:T(8,128)S(1)} %pad_maximum_fusion.refs_14_), channel_id=1, source_target_pairs={{0,48},{8,24},{2,50},{10,26},{4,52},{12,28},{6,54},{14,30},{16,32}... | collective-permute-start | bytes 3145736 | tf_op jit(solution)/shard_map/ppermute | solution.py:49
  37.6 10.3 %collective-permute-start.12 = (f32[32,16,256]{2,1,0:T(8,128)S(1)}, f32[32,16,256]{2,1,0:T(8,128)S(1)}, u32[]{:S(2)}, u32[]{:S(2)}) collective-permute-start(f32[32,16,256]{2,1,0:T(8,128)S(1)} %pad_maximum_fusion.3.refs_10_), channel_id=1, source_target_pairs={{0,8},{8,0},{2,10},{10,2},{4,12},{12,4},{6,14},{14,6},{16,24},{24,... | collective-permute-start | bytes 1572872 | tf_op jit(solution)/shard_map/ppermute | solution.py:49
  40.9 24.9 %copy-start.1 = (f32[32,16,384]{2,1,0:T(8,128)}, f32[32,16,384]{2,1,0:T(8,128)S(1)}, u32[]{:S(2)}) copy-start(f32[32,16,384]{2,1,0:T(8,128)S(1)} %pad_maximum_fusion.1.refs_2_) | copy-start | bytes 2359300
  40.9 15.7 %collective-permute-start.3 = (f32[32,16,384]{2,1,0:T(8,128)S(1)}, f32[32,16,384]{2,1,0:T(8,128)}, u32[]{:S(2)}, u32[]{:S(2)}) collective-permute-start(f32[32,16,384]{2,1,0:T(8,128)S(1)} %pad_maximum_fusion.1.refs_2_), channel_id=1, source_target_pairs={{0,6},{8,10},{2,4},{10,8},{4,2},{12,14},{6,0},{14,12},{16,22},{24,... | collective-permute-start | bytes 2359304 | tf_op jit(solution)/shard_map/ppermute | solution.py:49
  46.6 10.6 %collective-permute-start.2 = (f32[32,16,384]{2,1,0:T(8,128)S(1)}, f32[32,16,384]{2,1,0:T(8,128)S(1)}, u32[]{:S(2)}, u32[]{:S(2)}) collective-permute-start(f32[32,16,384]{2,1,0:T(8,128)S(1)} %pad_maximum_fusion.1.refs_2_), channel_id=1, source_target_pairs={{0,8},{8,0},{2,10},{10,2},{4,12},{12,4},{6,14},{14,6},{16,24},{24,... | collective-permute-start | bytes 2359304 | tf_op jit(solution)/shard_map/ppermute | solution.py:49
  46.6 19.1 %copy-start.2 = (f32[32,16,384]{2,1,0:T(8,128)}, f32[32,16,384]{2,1,0:T(8,128)S(1)}, u32[]{:S(2)}) copy-start(f32[32,16,384]{2,1,0:T(8,128)S(1)} %pad_maximum_fusion.2.refs_6_) | copy-start | bytes 2359300
  46.7 15.3 %collective-permute-start.8 = (f32[32,16,384]{2,1,0:T(8,128)S(1)}, f32[32,16,384]{2,1,0:T(8,128)}, u32[]{:S(2)}, u32[]{:S(2)}) collective-permute-start(f32[32,16,384]{2,1,0:T(8,128)S(1)} %pad_maximum_fusion.2.refs_6_), channel_id=1, source_target_pairs={{0,48},{8,24},{2,50},{10,26},{4,52},{12,28},{6,54},{14,30},{16,32}... | collective-permute-start | bytes 2359304 | tf_op jit(solution)/shard_map/ppermute | solution.py:49
  47.8 15.2 %copy-start.6 = (f32[32,16,256]{2,1,0:T(8,128)}, f32[32,16,256]{2,1,0:T(8,128)S(1)}, u32[]{:S(2)}) copy-start(f32[32,16,256]{2,1,0:T(8,128)S(1)} %collective-permute-done.12.refs_11_) | copy-start | bytes 1572868
  47.8 14.9 %collective-permute-start.7 = (f32[32,16,384]{2,1,0:T(8,128)S(1)}, f32[32,16,384]{2,1,0:T(8,128)S(1)}, u32[]{:S(2)}, u32[]{:S(2)}) collective-permute-start(f32[32,16,384]{2,1,0:T(8,128)S(1)} %pad_maximum_fusion.2.refs_6_), channel_id=1, source_target_pairs={{0,8},{8,0},{2,10},{10,2},{4,12},{12,4},{6,14},{14,6},{16,24},{24,... | collective-permute-start | bytes 2359304 | tf_op jit(solution)/shard_map/ppermute | solution.py:49
  56.6 7.6 %collective-permute-start.17 = (f32[4,2,2,64,256]{4,3,2,1,0:T(8,128)S(1)}, f32[4,2,2,64,256]{4,3,2,1,0:T(8,128)}, u32[]{:S(2)}, u32[]{:S(2)}) collective-permute-start(f32[4,2,2,64,256]{4,3,2,1,0:T(8,128)S(1)} %pad_maximum_fusion.refs_14_), channel_id=1, source_target_pairs={{0,8},{8,0},{2,10},{10,2},{4,12},{12,4},{6,14},{14,6},{16,24},{24,... | collective-permute-start | bytes 3145736 | tf_op jit(solution)/shard_map/ppermute | solution.py:49
  56.6 9.1 %collective-permute-start.19 = (f32[4,2,2,64,256]{4,3,2,1,0:T(8,128)}, f32[4,2,2,64,256]{4,3,2,1,0:T(8,128)}, u32[]{:S(2)}, u32[]{:S(2)}) collective-permute-start(f32[4,2,2,64,256]{4,3,2,1,0:T(8,128)} %collective-permute-done.18.refs_16_), channel_id=1, source_target_pairs={{0,8},{8,0},{2,10},{10,2},{4,12},{12,4},{6,14},{14,6},{16,24},{24,... | collective-permute-start | bytes 3145736 | tf_op jit(solution)/shard_map/ppermute | solution.py:49
  57.2 5.6 %copy-start.4 = (f32[32,16,384]{2,1,0:T(8,128)}, f32[32,16,384]{2,1,0:T(8,128)S(1)}, u32[]{:S(2)}) copy-start(f32[32,16,384]{2,1,0:T(8,128)S(1)} %collective-permute-done.2.refs_3_) | copy-start | bytes 2359300
  57.2 8.6 %collective-permute-start.4 = (f32[32,16,384]{2,1,0:T(8,128)}, f32[32,16,384]{2,1,0:T(8,128)}, u32[]{:S(2)}, u32[]{:S(2)}) collective-permute-start(f32[32,16,384]{2,1,0:T(8,128)} %collective-permute-done.3.refs_4_), channel_id=1, source_target_pairs={{0,8},{8,0},{2,10},{10,2},{4,12},{12,4},{6,14},{14,6},{16,24},{24,... | collective-permute-start | bytes 2359304 | tf_op jit(solution)/shard_map/ppermute | solution.py:49
  62.0 3.7 %collective-permute-start.9 = (f32[32,16,384]{2,1,0:T(8,128)}, f32[32,16,384]{2,1,0:T(8,128)}, u32[]{:S(2)}, u32[]{:S(2)}) collective-permute-start(f32[32,16,384]{2,1,0:T(8,128)} %collective-permute-done.8.refs_8_), channel_id=1, source_target_pairs={{0,8},{8,0},{2,10},{10,2},{4,12},{12,4},{6,14},{14,6},{16,24},{24,... | collective-permute-start | bytes 2359304 | tf_op jit(solution)/shard_map/ppermute | solution.py:49
  62.7 0.9 copy-start.5
  62.7 3.0 %collective-permute-start.14 = (f32[32,16,256]{2,1,0:T(8,128)}, f32[32,16,256]{2,1,0:T(8,128)}, u32[]{:S(2)}, u32[]{:S(2)}) collective-permute-start(f32[32,16,256]{2,1,0:T(8,128)} %collective-permute-done.13.refs_12_), channel_id=1, source_target_pairs={{0,8},{8,0},{2,10},{10,2},{4,12},{12,4},{6,14},{14,6},{16,24},{24,... | collective-permute-start | bytes 1572872 | tf_op jit(solution)/shard_map/ppermute | solution.py:49

commit v4 on v3

--- a/solution.py
+++ b/solution.py
@@ -17,8 +17,8 @@
 F_HIGH, F_LOW = 2.0**12, 2.0**21
 A_HIGH, A_LOW = 2.0**17, 2.0**26
 UNSCALE = 2.0**-38
-CUTS = (0, 384, 768, 1024)
-ORDERS = ("xyz", "yzx", "zxy")
+CUTS = (0, 512, 1024)
+ORDERS = ("xyz", "xzy")
 T_ORDER = ("y2", "x1", "x2")
 FIRST = (1, 3)
 SECOND = (3, 1)
@@ -304,9 +304,9 @@
 
 def gathered_fit(fit_bd):
     value = sent_to_all(fit_bd, cubes())
-    parts = [value[:, :, CUTS[i] : CUTS[i + 1]] for i in range(3)]
-    for at in range(2):
-        parts = [grown(part, order[at] + "2") for part, order in zip(parts, ORDERS)]
+    value = grown(value, "x2")
+    parts = [value[:, :, CUTS[i] : CUTS[i + 1]] for i in range(len(ORDERS))]
+    parts = [grown(part, order[1] + "2") for part, order in zip(parts, ORDERS)]
     arrived = [swap(part, order[2] + "2") for part, order in zip(parts, ORDERS)]
     near = [swap(part, "core") for part in parts]
     far = [swap(part, "core") for part in arrived]

time: 124 us -> 117 us (0.944)
  starting transfers between devices: 35.9 us -> 20.9 us
  blocking collectives: 23.2 us -> 34.2 us
  waiting for transfers between devices: 24.4 us -> 22.8 us
  local copies, waits for them, and re-layouts: 3.03 us -> 1.72 us
    all_to_all x0 -> x1, blocking collectives: none -> 13 us  [sent_to_all(): lax.all_to_all(copies, ('aa', 'col'), 0, 0, tiled=True, axis_index_groups...]
    ppermute x20 -> x14, starting transfers between devices: 30.7 us -> 20.9 us  [swap(): return lax.ppermute(value, ('aa', 'col'), flipped(move))]
    all_to_all x1 -> x0, starting transfers between devices: 5.22 us -> none  [sent_to_all(): lax.all_to_all(copies, ('aa', 'col'), 0, 0, tiled=True, axis_index_groups...]
    all_to_all x1 -> x0, waiting for transfers between devices: 4.85 us -> none  [sent_to_all(): lax.all_to_all(copies, ('aa', 'col'), 0, 0, tiled=True, axis_index_groups...]
    ppermute x20 -> x14, waiting for transfers between devices: 19.5 us -> 22.8 us  [swap(): return lax.ppermute(value, ('aa', 'col'), flipped(move))]
    all_to_all x1, blocking collectives: 23.2 us -> 21.2 us  [shards(): pieces = lax.all_to_all(pieces, 'col', 0, 0, tiled=True)]
  transfers between devices with their start and end apart: 21 -> 14, of which waited for: 7 -> 7; matrix products, arithmetic and copies ran while one was open for 2% -> 3% of each run, Pallas kernels for 0% -> 0%
where the time goes in v4:
time: 117 us
  blocking collectives  34.2 us (29%)
  Pallas kernels  34.1 us (29%)
  waiting for transfers between devices  22.8 us (19%)
  starting transfers between devices  20.9 us (18%)
  other arithmetic  2.85 us (2%)
  local copies, waits for them, and re-layouts  1.72 us (1%)
    pallas_call x1, Pallas kernels, contracted(): pl.pallas_call(functools.partial(kernel, n_fit=len(fits), n_amp=len(amps)...  34.1 us
    ppermute x14, waiting for transfers between devices, swap(): return lax.ppermute(value, ('aa', 'col'), flipped(move))  22.8 us
    all_to_all x1, blocking collectives, shards(): pieces = lax.all_to_all(pieces, 'col', 0, 0, tiled=True)  21.2 us
    ppermute x14, starting transfers between devices, swap(): return lax.ppermute(value, ('aa', 'col'), flipped(move))  20.9 us
    all_to_all x1, blocking collectives, sent_to_all(): lax.all_to_all(copies, ('aa', 'col'), 0, 0, tiled=True, axis_index_groups...  13 us
  transfers between devices with their start and end apart: 14, of which 7 were waited for; matrix products, arithmetic and copies ran while one was open for 3% of the time, Pallas kernels for 0%

profile of v4, /device:TPU:0, one launch (start us, length us, event | category | flops | bytes accessed | tf_op | source)
XLA Modules:
  0.0 116.7 jit_solution(14281480907049216105)
XLA Ops:
  0.0 0.9 broadcast_in_dim.6
  0.9 13.0 %all_to_all.10 = f32[8,16,1024]{2,1,0:T(8,128)S(1)} all-to-all(f32[8,16,1024]{2,1,0:T(8,128)S(1)} %broadcast_in_dim.6), channel_id=1, replica_groups={{0,2,1,3,16,18,17,19},{4,6,5,7,20,22,21,23},{64,66,65,67,80,82,81,83},{..., dimensions={0} | all-to-all | bytes 1048576 | tf_op jit(solution)/shard_map/all_to_all | solution.py:291
  13.9 2.2 %collective-permute-start = (f32[8,16,1024]{2,1,0:T(8,128)S(1)}, f32[8,16,1024]{2,1,0:T(8,128)S(1)}, u32[]{:S(2)}, u32[]{:S(2)}) collective-permute-start(f32[8,16,1024]{2,1,0:T(8,128)S(1)} %all_to_all.10), channel_id=1, source_target_pairs={{0,48},{8,24},{2,50},{10,26},{4,52},{12,28},{6,54},{14,30},{16,32}... | collective-permute-start | bytes 1572872 | tf_op jit(solution)/shard_map/ppermute | solution.py:49
  16.1 2.9 %collective-permute-start.9 = (f32[1,2,2,64,256]{4,3,2,1,0:T(8,128)}, f32[1,2,2,64,256]{4,3,2,1,0:T(8,128)S(1)}, u32[]{:S(2)}, u32[]{:S(2)}) collective-permute-start(f32[1,2,2,64,256]{4,3,2,1,0:T(8,128)} %bitcast.8), channel_id=1, source_target_pairs={{0,64},{8,72},{2,66},{10,74},{4,68},{12,76},{6,70},{14,78},{16,80}... | collective-permute-start | bytes 786440 | tf_op jit(solution)/shard_map/ppermute | solution.py:49
  19.0 5.9 %collective-permute-done.9 = f32[1,2,2,64,256]{4,3,2,1,0:T(8,128)S(1)} collective-permute-done((f32[1,2,2,64,256]{4,3,2,1,0:T(8,128)}, f32[1,2,2,64,256]{4,3,2,1,0:T(8,128)S(1)}, u32[]{:S(2)}, u32[]{:S(2)}) %collective-permute-start.9) | collective-permute-done | bytes 262176 | tf_op jit(solution)/shard_map/ppermute | solution.py:49
  24.9 1.0 pad_maximum_fusion.3
  25.9 0.1 collective-permute-start.10
  26.0 0.0 collective-permute-done
  26.1 0.1 fusion
  26.2 1.8 %collective-permute-start.1 = (f32[16,16,512]{2,1,0:T(8,128)S(1)}, f32[16,16,512]{2,1,0:T(8,128)S(1)}, u32[]{:S(2)}, u32[]{:S(2)}) collective-permute-start(f32[16,16,512]{2,1,0:T(8,128)S(1)} %get-tuple-element.6), channel_id=1, source_target_pairs={{0,65},{8,9},{2,67},{10,11},{4,69},{12,13},{6,71},{14,15},{16,81},... | collective-permute-start | bytes 1572872 | tf_op jit(solution)/shard_map/ppermute | solution.py:49
  28.0 4.6 %collective-permute-start.5 = (f32[16,16,512]{2,1,0:T(8,128)S(1)}, f32[16,16,512]{2,1,0:T(8,128)S(1)}, u32[]{:S(2)}, u32[]{:S(2)}) collective-permute-start(f32[16,16,512]{2,1,0:T(8,128)S(1)} %get-tuple-element.5), channel_id=1, source_target_pairs={{0,6},{8,10},{2,4},{10,8},{4,2},{12,14},{6,0},{14,12},{16,22},{24,... | collective-permute-start | bytes 1572872 | tf_op jit(solution)/shard_map/ppermute | solution.py:49
  32.6 2.6 %collective-permute-done.10 = f32[2,2,2,64,256]{4,3,2,1,0:T(8,128)S(1)} collective-permute-done((f32[2,2,2,64,256]{4,3,2,1,0:T(8,128)S(1)}, f32[2,2,2,64,256]{4,3,2,1,0:T(8,128)S(1)}, u32[]{:S(2)}, u32[]{:S(2)}) %collective-permute-start.10) | collective-permute-done | bytes 524320 | tf_op jit(solution)/shard_map/ppermute | solution.py:49
  35.2 1.0 pad_maximum_fusion.2.refs_10_
  36.2 0.0 copy-start
  36.2 1.3 %collective-permute-start.12 = (f32[4,2,2,64,256]{4,3,2,1,0:T(8,128)S(1)}, f32[4,2,2,64,256]{4,3,2,1,0:T(8,128)}, u32[]{:S(2)}, u32[]{:S(2)}) collective-permute-start(f32[4,2,2,64,256]{4,3,2,1,0:T(8,128)S(1)} %pad_maximum_fusion.2.refs_10_), channel_id=1, source_target_pairs={{0,48},{8,24},{2,50},{10,26},{4,52},{12,28},{6,54},{14,30},{16,32}... | collective-permute-start | bytes 3145736 | tf_op jit(solution)/shard_map/ppermute | solution.py:49
  37.5 2.2 %collective-permute-start.11 = (f32[4,2,2,64,256]{4,3,2,1,0:T(8,128)S(1)}, f32[4,2,2,64,256]{4,3,2,1,0:T(8,128)S(1)}, u32[]{:S(2)}, u32[]{:S(2)}) collective-permute-start(f32[4,2,2,64,256]{4,3,2,1,0:T(8,128)S(1)} %pad_maximum_fusion.2.refs_10_), channel_id=1, source_target_pairs={{0,8},{8,0},{2,10},{10,2},{4,12},{12,4},{6,14},{14,6},{16,24},{24,... | collective-permute-start | bytes 3145736 | tf_op jit(solution)/shard_map/ppermute | solution.py:49
  39.7 0.0 collective-permute-done.1
  39.7 0.1 pad_maximum_fusion.refs_2_
  39.8 0.0 copy-start.1
  39.9 1.3 %collective-permute-start.3 = (f32[32,16,512]{2,1,0:T(8,128)S(1)}, f32[32,16,512]{2,1,0:T(8,128)}, u32[]{:S(2)}, u32[]{:S(2)}) collective-permute-start(f32[32,16,512]{2,1,0:T(8,128)S(1)} %pad_maximum_fusion.refs_2_), channel_id=1, source_target_pairs={{0,6},{8,10},{2,4},{10,8},{4,2},{12,14},{6,0},{14,12},{16,22},{24,... | collective-permute-start | bytes 3145736 | tf_op jit(solution)/shard_map/ppermute | solution.py:49
  41.2 0.0 collective-permute-done.5
  41.2 0.1 pad_maximum_fusion.1.refs_6_
  41.3 0.0 copy-start.2
  41.3 3.2 %collective-permute-start.7 = (f32[32,16,512]{2,1,0:T(8,128)S(1)}, f32[32,16,512]{2,1,0:T(8,128)}, u32[]{:S(2)}, u32[]{:S(2)}) collective-permute-start(f32[32,16,512]{2,1,0:T(8,128)S(1)} %pad_maximum_fusion.1.refs_6_), channel_id=1, source_target_pairs={{0,65},{8,9},{2,67},{10,11},{4,69},{12,13},{6,71},{14,15},{16,81},... | collective-permute-start | bytes 3145736 | tf_op jit(solution)/shard_map/ppermute | solution.py:49
  44.6 0.0 collective-permute-start.2
  44.6 7.9 %collective-permute-done.12.refs_12_ = f32[4,2,2,64,256]{4,3,2,1,0:T(8,128)} collective-permute-done((f32[4,2,2,64,256]{4,3,2,1,0:T(8,128)S(1)}, f32[4,2,2,64,256]{4,3,2,1,0:T(8,128)}, u32[]{:S(2)}, u32[]{:S(2)}) %collective-permute-start.12) | collective-permute-done | bytes 1048608 | tf_op jit(solution)/shard_map/ppermute | solution.py:49
  52.4 1.1 collective-permute-start.6
  53.5 0.0 collective-permute-done.11.refs_11_
  53.5 0.0 copy-start.3
  53.5 0.1 collective-permute-start.13
  53.6 2.4 %collective-permute-done.3.refs_4_ = f32[32,16,512]{2,1,0:T(8,128)} collective-permute-done((f32[32,16,512]{2,1,0:T(8,128)S(1)}, f32[32,16,512]{2,1,0:T(8,128)}, u32[]{:S(2)}, u32[]{:S(2)}) %collective-permute-start.3) | collective-permute-done | bytes 1048608 | tf_op jit(solution)/shard_map/ppermute | solution.py:49
  56.0 0.0 collective-permute-start.4
  56.0 1.5 %collective-permute-done.7.refs_8_ = f32[32,16,512]{2,1,0:T(8,128)} collective-permute-done((f32[32,16,512]{2,1,0:T(8,128)S(1)}, f32[32,16,512]{2,1,0:T(8,128)}, u32[]{:S(2)}, u32[]{:S(2)}) %collective-permute-start.7) | collective-permute-done | bytes 1048608 | tf_op jit(solution)/shard_map/ppermute | solution.py:49
  57.5 0.0 copy-done.3
  57.5 0.0 collective-permute-start.8
  57.5 0.6 pad_add_fusion.refs_0_
  58.1 0.0 collective-permute-done.2.refs_3_
  58.1 0.0 collective-permute-done.6.refs_7_
  58.1 0.0 collective-permute-done.13.refs_13_
  58.1 1.1 collective-permute-done.4.refs_5_
  59.2 1.5 %collective-permute-done.8.refs_9_ = f32[32,16,512]{2,1,0:T(8,128)} collective-permute-done((f32[32,16,512]{2,1,0:T(8,128)}, f32[32,16,512]{2,1,0:T(8,128)}, u32[]{:S(2)}, u32[]{:S(2)}) %collective-permute-start.8) | collective-permute-done | bytes 1048608 | tf_op jit(solution)/shard_map/ppermute | solution.py:49
  60.7 0.0 copy-done
  60.7 0.0 copy-done.1
  60.7 0.0 copy-done.2
  60.7 34.1 %shard_map.37 = f32[16,2,32,256]{3,2,1,0:T(8,128)} custom-call(s32[4]{0:T(128)} %pad_add_fusion.refs_0_, f32[32,64,2048]{2,1,0:T(8,128)} %refs_1_.1, f32[32,16,512]{2,1,0:T(8,128)} %copy-done.1, f32[32,16,512]{2,1,0:T(8,128)} %collective-permute-done.2.refs_3_, f32[32,16,512]{2,1,0:T(8,128)} %collective-permute-done.3.refs_4_, ...), custom_call_target="tpu_custom_call" | custom-call | tf_op jit(solution)/shard_map/pallas_call | solution.py:279
  94.8 21.2 %all_to_all.11 = f32[8,2,2,32,256]{4,3,2,1,0:T(8,128)S(1)} all-to-all(f32[8,2,2,32,256]{4,3,2,1,0:T(8,128)} %bitcast.7), channel_id=1, replica_groups=mesh['aa'=16,'col'=8] {'col'}, dimensions={0} | all-to-all | bytes 2097152 | tf_op jit(solution)/shard_map/all_to_all | solution.py:333
  116.0 0.1 reduce_sum.9
  116.0 0.7 copy.4
  (2 shorter events, 0.1 us)
Async XLA Ops:
  13.9 12.1 %collective-permute-start = (f32[8,16,1024]{2,1,0:T(8,128)S(1)}, f32[8,16,1024]{2,1,0:T(8,128)S(1)}, u32[]{:S(2)}, u32[]{:S(2)}) collective-permute-start(f32[8,16,1024]{2,1,0:T(8,128)S(1)} %all_to_all.10), channel_id=1, source_target_pairs={{0,48},{8,24},{2,50},{10,26},{4,52},{12,28},{6,54},{14,30},{16,32}... | collective-permute-start | bytes 1572872 | tf_op jit(solution)/shard_map/ppermute | solution.py:49
  16.1 8.8 %collective-permute-start.9 = (f32[1,2,2,64,256]{4,3,2,1,0:T(8,128)}, f32[1,2,2,64,256]{4,3,2,1,0:T(8,128)S(1)}, u32[]{:S(2)}, u32[]{:S(2)}) collective-permute-start(f32[1,2,2,64,256]{4,3,2,1,0:T(8,128)} %bitcast.8), channel_id=1, source_target_pairs={{0,64},{8,72},{2,66},{10,74},{4,68},{12,76},{6,70},{14,78},{16,80}... | collective-permute-start | bytes 786440 | tf_op jit(solution)/shard_map/ppermute | solution.py:49
  25.9 9.3 %collective-permute-start.10 = (f32[2,2,2,64,256]{4,3,2,1,0:T(8,128)S(1)}, f32[2,2,2,64,256]{4,3,2,1,0:T(8,128)S(1)}, u32[]{:S(2)}, u32[]{:S(2)}) collective-permute-start(f32[2,2,2,64,256]{4,3,2,1,0:T(8,128)S(1)} %pad_maximum_fusion.3), channel_id=1, source_target_pairs={{0,16},{8,56},{2,18},{10,58},{4,20},{12,60},{6,22},{14,62},{16,0},... | collective-permute-start | bytes 1572872 | tf_op jit(solution)/shard_map/ppermute | solution.py:49
  26.2 13.5 %collective-permute-start.1 = (f32[16,16,512]{2,1,0:T(8,128)S(1)}, f32[16,16,512]{2,1,0:T(8,128)S(1)}, u32[]{:S(2)}, u32[]{:S(2)}) collective-permute-start(f32[16,16,512]{2,1,0:T(8,128)S(1)} %get-tuple-element.6), channel_id=1, source_target_pairs={{0,65},{8,9},{2,67},{10,11},{4,69},{12,13},{6,71},{14,15},{16,81},... | collective-permute-start | bytes 1572872 | tf_op jit(solution)/shard_map/ppermute | solution.py:49
  28.0 13.2 %collective-permute-start.5 = (f32[16,16,512]{2,1,0:T(8,128)S(1)}, f32[16,16,512]{2,1,0:T(8,128)S(1)}, u32[]{:S(2)}, u32[]{:S(2)}) collective-permute-start(f32[16,16,512]{2,1,0:T(8,128)S(1)} %get-tuple-element.5), channel_id=1, source_target_pairs={{0,6},{8,10},{2,4},{10,8},{4,2},{12,14},{6,0},{14,12},{16,22},{24,... | collective-permute-start | bytes 1572872 | tf_op jit(solution)/shard_map/ppermute | solution.py:49
  36.2 24.4 %copy-start = (f32[4,2,2,64,256]{4,3,2,1,0:T(8,128)}, f32[4,2,2,64,256]{4,3,2,1,0:T(8,128)S(1)}, u32[]{:S(2)}) copy-start(f32[4,2,2,64,256]{4,3,2,1,0:T(8,128)S(1)} %pad_maximum_fusion.2.refs_10_) | copy-start | bytes 3145732
  36.2 16.2 %collective-permute-start.12 = (f32[4,2,2,64,256]{4,3,2,1,0:T(8,128)S(1)}, f32[4,2,2,64,256]{4,3,2,1,0:T(8,128)}, u32[]{:S(2)}, u32[]{:S(2)}) collective-permute-start(f32[4,2,2,64,256]{4,3,2,1,0:T(8,128)S(1)} %pad_maximum_fusion.2.refs_10_), channel_id=1, source_target_pairs={{0,48},{8,24},{2,50},{10,26},{4,52},{12,28},{6,54},{14,30},{16,32}... | collective-permute-start | bytes 3145736 | tf_op jit(solution)/shard_map/ppermute | solution.py:49
  37.5 16.0 %collective-permute-start.11 = (f32[4,2,2,64,256]{4,3,2,1,0:T(8,128)S(1)}, f32[4,2,2,64,256]{4,3,2,1,0:T(8,128)S(1)}, u32[]{:S(2)}, u32[]{:S(2)}) collective-permute-start(f32[4,2,2,64,256]{4,3,2,1,0:T(8,128)S(1)} %pad_maximum_fusion.2.refs_10_), channel_id=1, source_target_pairs={{0,8},{8,0},{2,10},{10,2},{4,12},{12,4},{6,14},{14,6},{16,24},{24,... | collective-permute-start | bytes 3145736 | tf_op jit(solution)/shard_map/ppermute | solution.py:49
  39.8 20.8 %copy-start.1 = (f32[32,16,512]{2,1,0:T(8,128)}, f32[32,16,512]{2,1,0:T(8,128)S(1)}, u32[]{:S(2)}) copy-start(f32[32,16,512]{2,1,0:T(8,128)S(1)} %pad_maximum_fusion.refs_2_) | copy-start | bytes 3145732
  39.9 16.2 %collective-permute-start.3 = (f32[32,16,512]{2,1,0:T(8,128)S(1)}, f32[32,16,512]{2,1,0:T(8,128)}, u32[]{:S(2)}, u32[]{:S(2)}) collective-permute-start(f32[32,16,512]{2,1,0:T(8,128)S(1)} %pad_maximum_fusion.refs_2_), channel_id=1, source_target_pairs={{0,6},{8,10},{2,4},{10,8},{4,2},{12,14},{6,0},{14,12},{16,22},{24,... | collective-permute-start | bytes 3145736 | tf_op jit(solution)/shard_map/ppermute | solution.py:49
  41.3 19.4 %copy-start.2 = (f32[32,16,512]{2,1,0:T(8,128)}, f32[32,16,512]{2,1,0:T(8,128)S(1)}, u32[]{:S(2)}) copy-start(f32[32,16,512]{2,1,0:T(8,128)S(1)} %pad_maximum_fusion.1.refs_6_) | copy-start | bytes 3145732
  41.3 16.2 %collective-permute-start.7 = (f32[32,16,512]{2,1,0:T(8,128)S(1)}, f32[32,16,512]{2,1,0:T(8,128)}, u32[]{:S(2)}, u32[]{:S(2)}) collective-permute-start(f32[32,16,512]{2,1,0:T(8,128)S(1)} %pad_maximum_fusion.1.refs_6_), channel_id=1, source_target_pairs={{0,65},{8,9},{2,67},{10,11},{4,69},{12,13},{6,71},{14,15},{16,81},... | collective-permute-start | bytes 3145736 | tf_op jit(solution)/shard_map/ppermute | solution.py:49
  44.6 13.5 %collective-permute-start.2 = (f32[32,16,512]{2,1,0:T(8,128)S(1)}, f32[32,16,512]{2,1,0:T(8,128)}, u32[]{:S(2)}, u32[]{:S(2)}) collective-permute-start(f32[32,16,512]{2,1,0:T(8,128)S(1)} %pad_maximum_fusion.refs_2_), channel_id=1, source_target_pairs={{0,8},{8,0},{2,10},{10,2},{4,12},{12,4},{6,14},{14,6},{16,24},{24,... | collective-permute-start | bytes 3145736 | tf_op jit(solution)/shard_map/ppermute | solution.py:49
  52.4 5.7 %collective-permute-start.6 = (f32[32,16,512]{2,1,0:T(8,128)S(1)}, f32[32,16,512]{2,1,0:T(8,128)}, u32[]{:S(2)}, u32[]{:S(2)}) collective-permute-start(f32[32,16,512]{2,1,0:T(8,128)S(1)} %pad_maximum_fusion.1.refs_6_), channel_id=1, source_target_pairs={{0,8},{8,0},{2,10},{10,2},{4,12},{12,4},{6,14},{14,6},{16,24},{24,... | collective-permute-start | bytes 3145736 | tf_op jit(solution)/shard_map/ppermute | solution.py:49
  53.5 4.0 %copy-start.3 = (f32[4,2,2,64,256]{4,3,2,1,0:T(8,128)}, f32[4,2,2,64,256]{4,3,2,1,0:T(8,128)S(1)}, u32[]{:S(2)}) copy-start(f32[4,2,2,64,256]{4,3,2,1,0:T(8,128)S(1)} %collective-permute-done.11.refs_11_) | copy-start | bytes 3145732
  53.5 4.6 %collective-permute-start.13 = (f32[4,2,2,64,256]{4,3,2,1,0:T(8,128)}, f32[4,2,2,64,256]{4,3,2,1,0:T(8,128)}, u32[]{:S(2)}, u32[]{:S(2)}) collective-permute-start(f32[4,2,2,64,256]{4,3,2,1,0:T(8,128)} %collective-permute-done.12.refs_12_), channel_id=1, source_target_pairs={{0,8},{8,0},{2,10},{10,2},{4,12},{12,4},{6,14},{14,6},{16,24},{24,... | collective-permute-start | bytes 3145736 | tf_op jit(solution)/shard_map/ppermute | solution.py:49
  56.0 3.1 %collective-permute-start.4 = (f32[32,16,512]{2,1,0:T(8,128)}, f32[32,16,512]{2,1,0:T(8,128)}, u32[]{:S(2)}, u32[]{:S(2)}) collective-permute-start(f32[32,16,512]{2,1,0:T(8,128)} %collective-permute-done.3.refs_4_), channel_id=1, source_target_pairs={{0,8},{8,0},{2,10},{10,2},{4,12},{12,4},{6,14},{14,6},{16,24},{24,... | collective-permute-start | bytes 3145736 | tf_op jit(solution)/shard_map/ppermute | solution.py:49
  57.5 3.1 %collective-permute-start.8 = (f32[32,16,512]{2,1,0:T(8,128)}, f32[32,16,512]{2,1,0:T(8,128)}, u32[]{:S(2)}, u32[]{:S(2)}) collective-permute-start(f32[32,16,512]{2,1,0:T(8,128)} %collective-permute-done.7.refs_8_), channel_id=1, source_target_pairs={{0,8},{8,0},{2,10},{10,2},{4,12},{12,4},{6,14},{14,6},{16,24},{24,... | collective-permute-start | bytes 3145736 | tf_op jit(solution)/shard_map/ppermute | solution.py:49

commit v5 on v4

--- a/solution.py
+++ b/solution.py
@@ -302,8 +302,7 @@
     ]
 
 
-def gathered_fit(fit_bd):
-    value = sent_to_all(fit_bd, cubes())
+def gathered_fit(value):
     value = grown(value, "x2")
     parts = [value[:, :, CUTS[i] : CUTS[i + 1]] for i in range(len(ORDERS))]
     parts = [grown(part, order[1] + "2") for part, order in zip(parts, ORDERS)]
@@ -314,9 +313,7 @@
 
 
 def gathered_amplitudes(amplitudes):
-    value = amplitudes[None]
-    value = grown(value, "y2h")
-    value = grown(value, "x1")
+    value = grown(amplitudes, "x1")
     arrived = swap(value, "x2")
     return [value, swap(value, "core"), arrived, swap(arrived, "core")]
 
@@ -324,8 +321,11 @@
 def shards(fit_ac, fit_bd, amplitudes):
     x, y, z, core = position()
     where = jnp.stack([x, y, z, core]).astype(jnp.int32)
-    fits = gathered_fit(fit_bd)
-    amps = gathered_amplitudes(amplitudes)
+    near, doubled = lax.optimization_barrier(
+        (sent_to_all(fit_bd, cubes()), grown(amplitudes[None], "y2h"))
+    )
+    fits = gathered_fit(near)
+    amps = gathered_amplitudes(doubled)
     partial = contracted(where, fit_ac, fits, amps)
     b_size, k_size, a_size, pairs = partial.shape
     peers = lax.axis_size("col")

time: 117 us -> 127 us (1.085)
  waiting for transfers between devices: 22.8 us -> 37.4 us
  blocking collectives: 34.2 us -> 19.7 us
  starting transfers between devices: 20.9 us -> 30.8 us
    ppermute x14, waiting for transfers between devices: 22.8 us -> 37.4 us  [swap(): return lax.ppermute(value, ('aa', 'col'), flipped(move))]
    all_to_all x1 -> x0, blocking collectives: 13 us -> none  [sent_to_all(): lax.all_to_all(copies, ('aa', 'col'), 0, 0, tiled=True, axis_index_groups...]
    all_to_all x0 -> x1, starting transfers between devices: none -> 5.22 us  [sent_to_all(): lax.all_to_all(copies, ('aa', 'col'), 0, 0, tiled=True, axis_index_groups...]
    ppermute x14, starting transfers between devices: 20.9 us -> 25.6 us  [swap(): return lax.ppermute(value, ('aa', 'col'), flipped(move))]
    all_to_all x1, blocking collectives: 21.2 us -> 19.7 us  [shards(): pieces = lax.all_to_all(pieces, 'col', 0, 0, tiled=True)]
  transfers between devices with their start and end apart: 14 -> 15, of which waited for: 7 -> 6; matrix products, arithmetic and copies ran while one was open for 3% -> 2% of each run, Pallas kernels for 0% -> 0%
where the time goes in v5:
time: 127 us
  waiting for transfers between devices  37.4 us (29%)
  Pallas kernels  34.1 us (27%)
  starting transfers between devices  30.8 us (24%)
  blocking collectives  19.7 us (16%)
  local copies, waits for them, and re-layouts  2.61 us (2%)
  other arithmetic  1.92 us (2%)
    ppermute x14, waiting for transfers between devices, swap(): return lax.ppermute(value, ('aa', 'col'), flipped(move))  37.4 us
    pallas_call x1, Pallas kernels, contracted(): pl.pallas_call(functools.partial(kernel, n_fit=len(fits), n_amp=len(amps)...  34.1 us
    ppermute x14, starting transfers between devices, swap(): return lax.ppermute(value, ('aa', 'col'), flipped(move))  25.6 us
    all_to_all x1, blocking collectives, shards(): pieces = lax.all_to_all(pieces, 'col', 0, 0, tiled=True)  19.7 us
    all_to_all x1, starting transfers between devices, sent_to_all(): lax.all_to_all(copies, ('aa', 'col'), 0, 0, tiled=True, axis_index_groups...  5.22 us
  transfers between devices with their start and end apart: 15, of which 6 were waited for; matrix products, arithmetic and copies ran while one was open for 2% of the time, Pallas kernels for 0%

profile of v5, /device:TPU:0, one launch (start us, length us, event | category | flops | bytes accessed | tf_op | source)
XLA Modules:
  0.0 126.7 jit_solution(10665708724480347190)
XLA Ops:
  0.0 1.7 %broadcast_in_dim.6 = f32[8,16,1024]{2,1,0:T(8,128)} broadcast(f32[16,1024]{1,0:T(8,128)} %param.4), dimensions={1,2} | broadcast | bytes 589824 | tf_op jit(solution)/shard_map/broadcast_in_dim | solution.py:290
  1.7 5.2 %all-to-all-start = ((f32[8,16,1024]{2,1,0:T(8,128)}), f32[8,16,1024]{2,1,0:T(8,128)S(1)}, u32[]{:S(2)}, u32[]{:S(2)}) async-start(f32[8,16,1024]{2,1,0:T(8,128)} %broadcast_in_dim.6), calls=%async_computation | async-start | bytes 1048576 | tf_op jit(solution)/shard_map/all_to_all | solution.py:291
  6.9 2.9 %collective-permute-start = (f32[1,2,2,64,256]{4,3,2,1,0:T(8,128)}, f32[1,2,2,64,256]{4,3,2,1,0:T(8,128)S(1)}, u32[]{:S(2)}, u32[]{:S(2)}) collective-permute-start(f32[1,2,2,64,256]{4,3,2,1,0:T(8,128)} %bitcast.9), channel_id=1, source_target_pairs={{0,64},{8,72},{2,66},{10,74},{4,68},{12,76},{6,70},{14,78},{16,80}... | collective-permute-start | bytes 786440 | tf_op jit(solution)/shard_map/ppermute | solution.py:49
  9.8 10.4 %collective-permute-done = f32[1,2,2,64,256]{4,3,2,1,0:T(8,128)S(1)} collective-permute-done((f32[1,2,2,64,256]{4,3,2,1,0:T(8,128)}, f32[1,2,2,64,256]{4,3,2,1,0:T(8,128)S(1)}, u32[]{:S(2)}, u32[]{:S(2)}) %collective-permute-start) | collective-permute-done | bytes 262176 | tf_op jit(solution)/shard_map/ppermute | solution.py:49
  20.2 1.0 pad_maximum_fusion.2
  21.2 0.0 all-to-all-done
  21.2 2.6 %collective-permute-start.1 = (f32[8,16,1024]{2,1,0:T(8,128)S(1)}, f32[8,16,1024]{2,1,0:T(8,128)S(1)}, u32[]{:S(2)}, u32[]{:S(2)}) collective-permute-start(f32[8,16,1024]{2,1,0:T(8,128)S(1)} %all-to-all-done), channel_id=1, source_target_pairs={{0,48},{8,24},{2,50},{10,26},{4,52},{12,28},{6,54},{14,30},{16,32}... | collective-permute-start | bytes 1572872 | tf_op jit(solution)/shard_map/ppermute | solution.py:49
  23.8 0.7 collective-permute-start.10
  24.5 9.6 %collective-permute-done.1 = f32[8,16,1024]{2,1,0:T(8,128)S(1)} collective-permute-done((f32[8,16,1024]{2,1,0:T(8,128)S(1)}, f32[8,16,1024]{2,1,0:T(8,128)S(1)}, u32[]{:S(2)}, u32[]{:S(2)}) %collective-permute-start.1) | collective-permute-done | bytes 524320 | tf_op jit(solution)/shard_map/ppermute | solution.py:49
  34.1 0.1 fusion
  34.2 1.3 %collective-permute-start.2 = (f32[16,16,512]{2,1,0:T(8,128)S(1)}, f32[16,16,512]{2,1,0:T(8,128)S(1)}, u32[]{:S(2)}, u32[]{:S(2)}) collective-permute-start(f32[16,16,512]{2,1,0:T(8,128)S(1)} %get-tuple-element.10), channel_id=1, source_target_pairs={{0,65},{8,9},{2,67},{10,11},{4,69},{12,13},{6,71},{14,15},{16,81},... | collective-permute-start | bytes 1572872 | tf_op jit(solution)/shard_map/ppermute | solution.py:49
  35.5 7.1 %collective-permute-start.6 = (f32[16,16,512]{2,1,0:T(8,128)S(1)}, f32[16,16,512]{2,1,0:T(8,128)S(1)}, u32[]{:S(2)}, u32[]{:S(2)}) collective-permute-start(f32[16,16,512]{2,1,0:T(8,128)S(1)} %get-tuple-element.9), channel_id=1, source_target_pairs={{0,6},{8,10},{2,4},{10,8},{4,2},{12,14},{6,0},{14,12},{16,22},{24,... | collective-permute-start | bytes 1572872 | tf_op jit(solution)/shard_map/ppermute | solution.py:49
  42.7 0.0 collective-permute-done.10
  42.8 0.0 copy-start.2
  42.8 2.3 %collective-permute-start.12 = (f32[4,2,2,64,256]{4,3,2,1,0:T(8,128)S(1)}, f32[4,2,2,64,256]{4,3,2,1,0:T(8,128)}, u32[]{:S(2)}, u32[]{:S(2)}) collective-permute-start(f32[4,2,2,64,256]{4,3,2,1,0:T(8,128)S(1)} %constant_dynamic-update-slice_fusion.2.refs_10_), channel_id=1, source_target_pairs={{0,48},{8,24},{2,50},{10,26},{4,52},{12,28},{6,54},{14,30},{16,32}... | collective-permute-start | bytes 3145736 | tf_op jit(solution)/shard_map/ppermute | solution.py:49
  45.1 0.0 collective-permute-start.11
  45.1 0.0 collective-permute-done.2
  45.1 0.1 pad_maximum_fusion.refs_2_
  45.2 0.0 copy-start
  45.2 7.6 %collective-permute-start.4 = (f32[32,16,512]{2,1,0:T(8,128)S(1)}, f32[32,16,512]{2,1,0:T(8,128)}, u32[]{:S(2)}, u32[]{:S(2)}) collective-permute-start(f32[32,16,512]{2,1,0:T(8,128)S(1)} %pad_maximum_fusion.refs_2_), channel_id=1, source_target_pairs={{0,6},{8,10},{2,4},{10,8},{4,2},{12,14},{6,0},{14,12},{16,22},{24,... | collective-permute-start | bytes 3145736 | tf_op jit(solution)/shard_map/ppermute | solution.py:49
  52.8 0.0 collective-permute-done.6
  52.8 0.1 pad_maximum_fusion.1.refs_6_
  52.9 0.0 copy-start.1
  52.9 0.5 collective-permute-start.8
  53.5 0.0 collective-permute-start.3
  53.5 5.5 %collective-permute-done.12.refs_12_ = f32[4,2,2,64,256]{4,3,2,1,0:T(8,128)} collective-permute-done((f32[4,2,2,64,256]{4,3,2,1,0:T(8,128)S(1)}, f32[4,2,2,64,256]{4,3,2,1,0:T(8,128)}, u32[]{:S(2)}, u32[]{:S(2)}) %collective-permute-start.12) | collective-permute-done | bytes 1048608 | tf_op jit(solution)/shard_map/ppermute | solution.py:49
  59.0 0.0 collective-permute-start.7
  59.0 0.0 collective-permute-done.11.refs_11_
  59.0 0.0 copy-start.3
  59.0 0.5 collective-permute-start.13
  59.5 6.2 %collective-permute-done.4.refs_4_ = f32[32,16,512]{2,1,0:T(8,128)} collective-permute-done((f32[32,16,512]{2,1,0:T(8,128)S(1)}, f32[32,16,512]{2,1,0:T(8,128)}, u32[]{:S(2)}, u32[]{:S(2)}) %collective-permute-start.4) | collective-permute-done | bytes 1048608 | tf_op jit(solution)/shard_map/ppermute | solution.py:49
  65.7 0.0 collective-permute-start.5
  65.7 3.4 %collective-permute-done.8.refs_8_ = f32[32,16,512]{2,1,0:T(8,128)} collective-permute-done((f32[32,16,512]{2,1,0:T(8,128)S(1)}, f32[32,16,512]{2,1,0:T(8,128)}, u32[]{:S(2)}, u32[]{:S(2)}) %collective-permute-start.8) | collective-permute-done | bytes 1048608 | tf_op jit(solution)/shard_map/ppermute | solution.py:49
  69.1 0.0 copy-done.3
  69.1 0.0 collective-permute-start.9
  69.1 0.7 pad_add_fusion.refs_0_
  69.8 0.0 collective-permute-done.3.refs_3_
  69.8 0.0 collective-permute-done.7.refs_7_
  69.8 0.0 collective-permute-done.13.refs_13_
  69.8 0.0 collective-permute-done.5.refs_5_
  69.8 2.3 %collective-permute-done.9.refs_9_ = f32[32,16,512]{2,1,0:T(8,128)} collective-permute-done((f32[32,16,512]{2,1,0:T(8,128)}, f32[32,16,512]{2,1,0:T(8,128)}, u32[]{:S(2)}, u32[]{:S(2)}) %collective-permute-start.9) | collective-permute-done | bytes 1048608 | tf_op jit(solution)/shard_map/ppermute | solution.py:49
  72.1 0.0 copy-done.2
  72.1 0.0 copy-done
  72.1 0.0 copy-done.1
  72.1 34.1 %shard_map.37 = f32[16,2,32,256]{3,2,1,0:T(8,128)} custom-call(s32[4]{0:T(128)} %pad_add_fusion.refs_0_, f32[32,64,2048]{2,1,0:T(8,128)} %refs_1_.1, f32[32,16,512]{2,1,0:T(8,128)} %copy-done, f32[32,16,512]{2,1,0:T(8,128)} %collective-permute-done.3.refs_3_, f32[32,16,512]{2,1,0:T(8,128)} %collective-permute-done.4.refs_4_, ...), custom_call_target="tpu_custom_call" | custom-call | tf_op jit(solution)/shard_map/pallas_call | solution.py:279
  106.3 19.7 %all_to_all.10 = f32[8,2,2,32,256]{4,3,2,1,0:T(8,128)S(1)} all-to-all(f32[8,2,2,32,256]{4,3,2,1,0:T(8,128)} %bitcast.7), channel_id=1, replica_groups=mesh['aa'=16,'col'=8] {'col'}, dimensions={0} | all-to-all | bytes 2097152 | tf_op jit(solution)/shard_map/all_to_all | solution.py:333
  126.0 0.1 reduce_sum.9
  126.1 0.7 copy.4
  (4 shorter events, 0.1 us)
Async XLA Ops:
  1.7 19.5 %all-to-all-start = ((f32[8,16,1024]{2,1,0:T(8,128)}), f32[8,16,1024]{2,1,0:T(8,128)S(1)}, u32[]{:S(2)}, u32[]{:S(2)}) async-start(f32[8,16,1024]{2,1,0:T(8,128)} %broadcast_in_dim.6), calls=%async_computation | async-start | bytes 1048576 | tf_op jit(solution)/shard_map/all_to_all | solution.py:291
  6.9 13.3 %collective-permute-start = (f32[1,2,2,64,256]{4,3,2,1,0:T(8,128)}, f32[1,2,2,64,256]{4,3,2,1,0:T(8,128)S(1)}, u32[]{:S(2)}, u32[]{:S(2)}) collective-permute-start(f32[1,2,2,64,256]{4,3,2,1,0:T(8,128)} %bitcast.9), channel_id=1, source_target_pairs={{0,64},{8,72},{2,66},{10,74},{4,68},{12,76},{6,70},{14,78},{16,80}... | collective-permute-start | bytes 786440 | tf_op jit(solution)/shard_map/ppermute | solution.py:49
  21.2 12.9 %collective-permute-start.1 = (f32[8,16,1024]{2,1,0:T(8,128)S(1)}, f32[8,16,1024]{2,1,0:T(8,128)S(1)}, u32[]{:S(2)}, u32[]{:S(2)}) collective-permute-start(f32[8,16,1024]{2,1,0:T(8,128)S(1)} %all-to-all-done), channel_id=1, source_target_pairs={{0,48},{8,24},{2,50},{10,26},{4,52},{12,28},{6,54},{14,30},{16,32}... | collective-permute-start | bytes 1572872 | tf_op jit(solution)/shard_map/ppermute | solution.py:49
  23.8 18.9 %collective-permute-start.10 = (f32[2,2,2,64,256]{4,3,2,1,0:T(8,128)S(1)}, f32[2,2,2,64,256]{4,3,2,1,0:T(8,128)S(1)}, u32[]{:S(2)}, u32[]{:S(2)}) collective-permute-start(f32[2,2,2,64,256]{4,3,2,1,0:T(8,128)S(1)} %pad_maximum_fusion.2), channel_id=1, source_target_pairs={{0,16},{8,56},{2,18},{10,58},{4,20},{12,60},{6,22},{14,62},{16,0},... | collective-permute-start | bytes 1572872 | tf_op jit(solution)/shard_map/ppermute | solution.py:49
  34.2 10.9 %collective-permute-start.2 = (f32[16,16,512]{2,1,0:T(8,128)S(1)}, f32[16,16,512]{2,1,0:T(8,128)S(1)}, u32[]{:S(2)}, u32[]{:S(2)}) collective-permute-start(f32[16,16,512]{2,1,0:T(8,128)S(1)} %get-tuple-element.10), channel_id=1, source_target_pairs={{0,65},{8,9},{2,67},{10,11},{4,69},{12,13},{6,71},{14,15},{16,81},... | collective-permute-start | bytes 1572872 | tf_op jit(solution)/shard_map/ppermute | solution.py:49
  35.5 17.3 %collective-permute-start.6 = (f32[16,16,512]{2,1,0:T(8,128)S(1)}, f32[16,16,512]{2,1,0:T(8,128)S(1)}, u32[]{:S(2)}, u32[]{:S(2)}) collective-permute-start(f32[16,16,512]{2,1,0:T(8,128)S(1)} %get-tuple-element.9), channel_id=1, source_target_pairs={{0,6},{8,10},{2,4},{10,8},{4,2},{12,14},{6,0},{14,12},{16,22},{24,... | collective-permute-start | bytes 1572872 | tf_op jit(solution)/shard_map/ppermute | solution.py:49
  42.8 29.4 %copy-start.2 = (f32[4,2,2,64,256]{4,3,2,1,0:T(8,128)}, f32[4,2,2,64,256]{4,3,2,1,0:T(8,128)S(1)}, u32[]{:S(2)}) copy-start(f32[4,2,2,64,256]{4,3,2,1,0:T(8,128)S(1)} %constant_dynamic-update-slice_fusion.2.refs_10_) | copy-start | bytes 3145732
  42.8 16.2 %collective-permute-start.12 = (f32[4,2,2,64,256]{4,3,2,1,0:T(8,128)S(1)}, f32[4,2,2,64,256]{4,3,2,1,0:T(8,128)}, u32[]{:S(2)}, u32[]{:S(2)}) collective-permute-start(f32[4,2,2,64,256]{4,3,2,1,0:T(8,128)S(1)} %constant_dynamic-update-slice_fusion.2.refs_10_), channel_id=1, source_target_pairs={{0,48},{8,24},{2,50},{10,26},{4,52},{12,28},{6,54},{14,30},{16,32}... | collective-permute-start | bytes 3145736 | tf_op jit(solution)/shard_map/ppermute | solution.py:49
  45.1 13.9 %collective-permute-start.11 = (f32[4,2,2,64,256]{4,3,2,1,0:T(8,128)S(1)}, f32[4,2,2,64,256]{4,3,2,1,0:T(8,128)S(1)}, u32[]{:S(2)}, u32[]{:S(2)}) collective-permute-start(f32[4,2,2,64,256]{4,3,2,1,0:T(8,128)S(1)} %constant_dynamic-update-slice_fusion.2.refs_10_), channel_id=1, source_target_pairs={{0,8},{8,0},{2,10},{10,2},{4,12},{12,4},{6,14},{14,6},{16,24},{24,... | collective-permute-start | bytes 3145736 | tf_op jit(solution)/shard_map/ppermute | solution.py:49
  45.2 26.9 %copy-start = (f32[32,16,512]{2,1,0:T(8,128)}, f32[32,16,512]{2,1,0:T(8,128)S(1)}, u32[]{:S(2)}) copy-start(f32[32,16,512]{2,1,0:T(8,128)S(1)} %pad_maximum_fusion.refs_2_) | copy-start | bytes 3145732
  45.2 20.5 %collective-permute-start.4 = (f32[32,16,512]{2,1,0:T(8,128)S(1)}, f32[32,16,512]{2,1,0:T(8,128)}, u32[]{:S(2)}, u32[]{:S(2)}) collective-permute-start(f32[32,16,512]{2,1,0:T(8,128)S(1)} %pad_maximum_fusion.refs_2_), channel_id=1, source_target_pairs={{0,6},{8,10},{2,4},{10,8},{4,2},{12,14},{6,0},{14,12},{16,22},{24,... | collective-permute-start | bytes 3145736 | tf_op jit(solution)/shard_map/ppermute | solution.py:49
  52.9 19.2 %copy-start.1 = (f32[32,16,512]{2,1,0:T(8,128)}, f32[32,16,512]{2,1,0:T(8,128)S(1)}, u32[]{:S(2)}) copy-start(f32[32,16,512]{2,1,0:T(8,128)S(1)} %pad_maximum_fusion.1.refs_6_) | copy-start | bytes 3145732
  52.9 16.2 %collective-permute-start.8 = (f32[32,16,512]{2,1,0:T(8,128)S(1)}, f32[32,16,512]{2,1,0:T(8,128)}, u32[]{:S(2)}, u32[]{:S(2)}) collective-permute-start(f32[32,16,512]{2,1,0:T(8,128)S(1)} %pad_maximum_fusion.1.refs_6_), channel_id=1, source_target_pairs={{0,65},{8,9},{2,67},{10,11},{4,69},{12,13},{6,71},{14,15},{16,81},... | collective-permute-start | bytes 3145736 | tf_op jit(solution)/shard_map/ppermute | solution.py:49
  53.5 16.3 %collective-permute-start.3 = (f32[32,16,512]{2,1,0:T(8,128)S(1)}, f32[32,16,512]{2,1,0:T(8,128)}, u32[]{:S(2)}, u32[]{:S(2)}) collective-permute-start(f32[32,16,512]{2,1,0:T(8,128)S(1)} %pad_maximum_fusion.refs_2_), channel_id=1, source_target_pairs={{0,8},{8,0},{2,10},{10,2},{4,12},{12,4},{6,14},{14,6},{16,24},{24,... | collective-permute-start | bytes 3145736 | tf_op jit(solution)/shard_map/ppermute | solution.py:49
  59.0 10.8 %collective-permute-start.7 = (f32[32,16,512]{2,1,0:T(8,128)S(1)}, f32[32,16,512]{2,1,0:T(8,128)}, u32[]{:S(2)}, u32[]{:S(2)}) collective-permute-start(f32[32,16,512]{2,1,0:T(8,128)S(1)} %pad_maximum_fusion.1.refs_6_), channel_id=1, source_target_pairs={{0,8},{8,0},{2,10},{10,2},{4,12},{12,4},{6,14},{14,6},{16,24},{24,... | collective-permute-start | bytes 3145736 | tf_op jit(solution)/shard_map/ppermute | solution.py:49
  59.0 10.2 %copy-start.3 = (f32[4,2,2,64,256]{4,3,2,1,0:T(8,128)}, f32[4,2,2,64,256]{4,3,2,1,0:T(8,128)S(1)}, u32[]{:S(2)}) copy-start(f32[4,2,2,64,256]{4,3,2,1,0:T(8,128)S(1)} %collective-permute-done.11.refs_11_) | copy-start | bytes 3145732
  59.0 10.8 %collective-permute-start.13 = (f32[4,2,2,64,256]{4,3,2,1,0:T(8,128)}, f32[4,2,2,64,256]{4,3,2,1,0:T(8,128)}, u32[]{:S(2)}, u32[]{:S(2)}) collective-permute-start(f32[4,2,2,64,256]{4,3,2,1,0:T(8,128)} %collective-permute-done.12.refs_12_), channel_id=1, source_target_pairs={{0,8},{8,0},{2,10},{10,2},{4,12},{12,4},{6,14},{14,6},{16,24},{24,... | collective-permute-start | bytes 3145736 | tf_op jit(solution)/shard_map/ppermute | solution.py:49
  65.7 4.1 %collective-permute-start.5 = (f32[32,16,512]{2,1,0:T(8,128)}, f32[32,16,512]{2,1,0:T(8,128)}, u32[]{:S(2)}, u32[]{:S(2)}) collective-permute-start(f32[32,16,512]{2,1,0:T(8,128)} %collective-permute-done.4.refs_4_), channel_id=1, source_target_pairs={{0,8},{8,0},{2,10},{10,2},{4,12},{12,4},{6,14},{14,6},{16,24},{24,... | collective-permute-start | bytes 3145736 | tf_op jit(solution)/shard_map/ppermute | solution.py:49
  69.1 3.0 %collective-permute-start.9 = (f32[32,16,512]{2,1,0:T(8,128)}, f32[32,16,512]{2,1,0:T(8,128)}, u32[]{:S(2)}, u32[]{:S(2)}) collective-permute-start(f32[32,16,512]{2,1,0:T(8,128)} %collective-permute-done.8.refs_8_), channel_id=1, source_target_pairs={{0,8},{8,0},{2,10},{10,2},{4,12},{12,4},{6,14},{14,6},{16,24},{24,... | collective-permute-start | bytes 3145736 | tf_op jit(solution)/shard_map/ppermute | solution.py:49
